TPU v7x, 32 devices: a whole 2x2x4 slice. The times are simulated.
32 devices in a mesh: freq: 8 (over y, x, core), rcv: 4 (over z).
Axes of the slice: x: 2, y: 2, z: 4, core: 2. Of those that a mesh axis runs over, the one named last changes fastest.
Arguments:
- kernel: float32 [2, 128, 1024, 1024], P(None, 'freq', 'rcv'), may hold values from -2 to 2, as said below
- focus_start: float32 [8, 1024, 512], P('freq', 'rcv'), may hold values from -6 to 6
- onset: int32 [8, 1024], P('freq', 'rcv'), may hold values from 64 to 447
- freq_order: int32 [128], replicated, may hold values from 0 to 127, each once
Outputs:
- focusing: float32 [8, 1024, 512], P('freq', 'rcv')
- downgoing: float32 [8, 1024, 512], P('freq', 'rcv')
Inputs may be any that keep to these rules, and one draw needn't show every extreme that they name: kernel[c,k,s,r] equals kernel[c,k,r,s] exactly (reciprocity).
All inputs are finite; a program needn't handle non-finite values.
Results may differ from a plain program's by a relative error of at most 0.0001.
Values sent between devices are 32-bit elements; how exact they have to be, the bound alone decides.
No kernel may reach another device: no remote copies, remote signals or barrier semaphores. Data moves between devices by JAX's collectives and lax.ppermute only.
A program may use at most 128 MiB of HBM per device.

v0:
```python
import math

import jax
import jax.numpy as jnp
from jax import lax
from jax.sharding import PartitionSpec as P

ITERS = 2


def make_tables(freq_order, samples):
    sample_ids = jnp.arange(samples, dtype=jnp.int32)
    phase_ids = freq_order[:, None] * sample_ids[None, :] % samples
    angles = 2.0 * math.pi / samples * phase_ids.astype(jnp.float32)
    forward = jnp.stack([jnp.cos(angles), -jnp.sin(angles)])
    weights = jnp.where(freq_order == 0, 1.0, 2.0).astype(jnp.float32) / samples
    inverse_operator = forward * weights[None, :, None]
    return (forward, inverse_operator)


def complex_product(left, right, sign_parity, form):
    real_part = jnp.einsum(
        form, left[0], right[0], precision=lax.Precision.HIGHEST
    ) - sign_parity * jnp.einsum(form, left[1], right[1], precision=lax.Precision.HIGHEST)
    imag_part = sign_parity * jnp.einsum(
        form, left[0], right[1], precision=lax.Precision.HIGHEST
    ) + jnp.einsum(form, left[1], right[0], precision=lax.Precision.HIGHEST)
    return jnp.stack([real_part, imag_part])


def body(kernel, focus_start, onset, freq_order):
    samples = focus_start.shape[2]
    forward, inverse_operator = make_tables(freq_order, samples)
    window_mask = lax.broadcasted_iota(jnp.int32, focus_start.shape, 2) < onset[:, :, None]

    def multiply(spectral_field, sign_parity):
        partial_terms = complex_product(spectral_field, kernel, sign_parity, "fvr,frs->fvs")
        return lax.psum_scatter(partial_terms, "rcv", scatter_dimension=3, tiled=True)

    def convolve(traces, sign_parity):
        spectral_field = jnp.einsum(
            "ckt,vrt->ckvr", forward, traces, precision=lax.Precision.HIGHEST
        )
        spectral_field = lax.all_to_all(
            spectral_field, "freq", split_axis=1, concat_axis=2, tiled=True
        )
        kernel_product = multiply(spectral_field, sign_parity)
        returned_field = lax.all_to_all(
            kernel_product, "freq", split_axis=2, concat_axis=1, tiled=True
        )
        wavelet_signal = jnp.einsum(
            "uglq,ugi->lqi", returned_field, inverse_operator, precision=lax.Precision.HIGHEST
        )
        return jnp.where(window_mask, wavelet_signal, jnp.zeros_like(wavelet_signal))

    focusing = focus_start
    downgoing = focus_start
    for iteration in range(ITERS):
        downgoing = convolve(focusing, 1.0)
        focusing = focus_start + convolve(downgoing, -1.0)
    return (focusing, downgoing)


def solution(mesh):
    in_specs = (P(None, "freq", "rcv", None), P("freq", "rcv", None), P("freq", "rcv"), P())
    out_specs = (P("freq", "rcv", None), P("freq", "rcv", None))
    return jax.shard_map(body, mesh=mesh, in_specs=in_specs, out_specs=out_specs, check_vma=False)
```

profile of v0, /device:TPU:0, one launch (start us, length us, event | category | flops | bytes accessed | tf_op | source)
XLA Modules:
  0.0 400.5 jit_solution(3685458293791122430)
XLA Ops:
  7.2 1.8 fusion.134
  9.0 1.7 convolution_bitcast_fusion.7
  10.9 11.9 %all_to_all.120 = f32[2,128,1,256]{3,0,2,1:T(2,128)S(1)} all-to-all(f32[2,128,1,256]{3,0,2,1:T(2,128)S(1)} %copy.37), channel_id=1, replica_groups=mesh['freq'=8,'rcv'=4] {'freq'}, dimensions={1} | all-to-all | bytes 524288 | tf_op jit(solution)/shard_map/all_to_all | solution.py:44
  22.9 11.5 %fusion.12 = f32[16,8,1024]{2,1,0:T(8,128)S(1)} fusion(f32[2,16,256,1024]{3,2,1,0:T(8,128)} %param.4, f32[2,16,8,1,256]{4,2,1,3,0:T(8,128)S(1)} %bitcast.224), kind=kOutput, calls=%fused_computation.12 | convolution fusion | flops 402653184 | bytes 17432576 | tf_op jit(solution)/shard_map/fvr,frs->fvs/dot_general | solution.py:25
  34.4 11.5 %fusion.14 = f32[16,8,1024]{2,1,0:T(8,128)S(1)} fusion(f32[2,16,256,1024]{3,2,1,0:T(8,128)} %param.4, f32[2,16,8,1,256]{4,2,1,3,0:T(8,128)S(1)} %bitcast.225), kind=kOutput, calls=%fused_computation.14 | convolution fusion | flops 402653184 | bytes 17432576 | tf_op jit(solution)/shard_map/fvr,frs->fvs/dot_general | solution.py:24
  45.9 11.9 %fusion.57 = f32[1,16,8,1024]{3,2,1,0:T(8,128)S(1)} fusion(f32[16,8,1024]{2,1,0:T(8,128)S(1)} %fusion.12, f32[2,16,256,1024]{3,2,1,0:T(8,128)} %param.4, f32[2,16,8,1,256]{4,2,1,3,0:T(8,128)S(1)} %bitcast.226), kind=kOutput, calls=%fused_computation.55 | convolution fusion | flops 402784256 | bytes 17956864 | tf_op jit(solution)/shard_map/fvr,frs->fvs/dot_general | solution.py:27
  57.8 11.5 %fusion.51 = f32[1,16,8,1024]{3,2,1,0:T(8,128)S(1)} fusion(f32[16,8,1024]{2,1,0:T(8,128)S(1)} %fusion.14, f32[2,16,256,1024]{3,2,1,0:T(8,128)} %param.4, f32[2,16,8,1,256]{4,2,1,3,0:T(8,128)S(1)} %bitcast.227), kind=kOutput, calls=%fused_computation.53 | convolution fusion | flops 402784256 | bytes 17956864 | tf_op jit(solution)/shard_map/fvr,frs->fvs/dot_general | solution.py:22
  70.4 26.8 %reduce-scatter.5.cloned.1.call-done = f32[2,16,8,256]{3,2,1,0:T(8,128)} async-done(((f32[2,16,8,1024]{3,2,1,0:T(8,128)}), f32[2,16,8,256]{3,2,1,0:T(8,128)}) %reduce-scatter.5.cloned.1.call-update) | async-done | bytes 262160 | tf_op jit(solution)/shard_map/reduce_scatter | solution.py:38
  97.2 1.7 copy.40
  98.9 3.7 all-to-all-start.1
  102.7 6.8 %all-to-all-done.1 = f32[2,16,8,256]{3,1,0,2:T(8,128)S(1)} async-done(((f32[2,16,8,256]{3,1,0,2:T(8,128)}), f32[2,16,8,256]{3,1,0,2:T(8,128)S(1)}, u32[]{:S(2)}, u32[]{:S(2)}) %all-to-all-start.1) | async-done | bytes 262176 | tf_op jit(solution)/shard_map/all_to_all | solution.py:48
  111.1 9.5 %all_to_all.121 = f32[2,128,1,256]{3,0,2,1:T(2,128)S(1)} all-to-all(f32[2,128,1,256]{3,0,2,1:T(2,128)S(1)} %copy.43), channel_id=1, replica_groups=mesh['freq'=8,'rcv'=4] {'freq'}, dimensions={1} | all-to-all | bytes 524288 | tf_op jit(solution)/shard_map/all_to_all | solution.py:44
  120.8 11.5 %fusion.99 = f32[16,8,1024]{2,1,0:T(8,128)S(1)} fusion(f32[2,16,256,1024]{3,2,1,0:T(8,128)} %param.4, f32[2,16,8,1,256]{4,2,1,3,0:T(8,128)S(1)} %bitcast.228), kind=kOutput, calls=%fused_computation.69 | convolution fusion | flops 402784256 | bytes 17432576 | tf_op jit(solution)/shard_map/fvr,frs->fvs/dot_general | solution.py:25
  132.3 11.5 %fusion.96 = f32[16,8,1024]{2,1,0:T(8,128)S(1)} fusion(f32[2,16,256,1024]{3,2,1,0:T(8,128)} %param.4, f32[2,16,8,1,256]{4,2,1,3,0:T(8,128)S(1)} %bitcast.229), kind=kOutput, calls=%fused_computation.68 | convolution fusion | flops 402784256 | bytes 17432576 | tf_op jit(solution)/shard_map/fvr,frs->fvs/dot_general | solution.py:24
  143.8 11.7 %fusion.69 = f32[1,16,8,1024]{3,2,1,0:T(8,128)S(1)} fusion(f32[16,8,1024]{2,1,0:T(8,128)S(1)} %fusion.99, f32[2,16,256,1024]{3,2,1,0:T(8,128)} %param.4, f32[2,16,8,1,256]{4,2,1,3,0:T(8,128)S(1)} %bitcast.230), kind=kOutput, calls=%fused_computation.59 | convolution fusion | flops 402784256 | bytes 17956864 | tf_op jit(solution)/shard_map/fvr,frs->fvs/dot_general | solution.py:27
  155.5 11.5 %fusion.63 = f32[1,16,8,1024]{3,2,1,0:T(8,128)S(1)} fusion(f32[16,8,1024]{2,1,0:T(8,128)S(1)} %fusion.96, f32[2,16,256,1024]{3,2,1,0:T(8,128)} %param.4, f32[2,16,8,1,256]{4,2,1,3,0:T(8,128)S(1)} %bitcast.231), kind=kOutput, calls=%fused_computation.57 | convolution fusion | flops 402784256 | bytes 17956864 | tf_op jit(solution)/shard_map/fvr,frs->fvs/dot_general | solution.py:22
  168.1 24.1 %reduce-scatter.7.cloned.1.call-done = f32[2,16,8,256]{3,2,1,0:T(8,128)} async-done(((f32[2,16,8,1024]{3,2,1,0:T(8,128)}), f32[2,16,8,256]{3,2,1,0:T(8,128)}) %reduce-scatter.7.cloned.1.call-update) | async-done | bytes 262160 | tf_op jit(solution)/shard_map/reduce_scatter | solution.py:38
  193.2 10.4 %all_to_all.122 = f32[2,16,8,256]{3,1,0,2:T(8,128)S(1)} all-to-all(f32[2,16,8,256]{3,1,0,2:T(8,128)S(1)} %copy.46), channel_id=1, replica_groups=mesh['freq'=8,'rcv'=4] {'freq'}, dimensions={2} | all-to-all | bytes 524288 | tf_op jit(solution)/shard_map/all_to_all | solution.py:48
  205.3 9.7 %all_to_all.123 = f32[2,128,1,256]{3,0,2,1:T(2,128)S(1)} all-to-all(f32[2,128,1,256]{3,0,2,1:T(2,128)S(1)} %copy.49), channel_id=1, replica_groups=mesh['freq'=8,'rcv'=4] {'freq'}, dimensions={1} | all-to-all | bytes 524288 | tf_op jit(solution)/shard_map/all_to_all | solution.py:44
  215.1 11.5 %fusion.4 = f32[16,8,1024]{2,1,0:T(8,128)S(1)} fusion(f32[2,16,256,1024]{3,2,1,0:T(8,128)} %param.4, f32[2,16,8,1,256]{4,2,1,3,0:T(8,128)S(1)} %bitcast.232), kind=kOutput, calls=%fused_computation.4 | convolution fusion | flops 402653184 | bytes 17432576 | tf_op jit(solution)/shard_map/fvr,frs->fvs/dot_general | solution.py:25
  226.6 11.5 %fusion.6 = f32[16,8,1024]{2,1,0:T(8,128)S(1)} fusion(f32[2,16,256,1024]{3,2,1,0:T(8,128)} %param.4, f32[2,16,8,1,256]{4,2,1,3,0:T(8,128)S(1)} %bitcast.233), kind=kOutput, calls=%fused_computation.6 | convolution fusion | flops 402653184 | bytes 17432576 | tf_op jit(solution)/shard_map/fvr,frs->fvs/dot_general | solution.py:24
  238.1 11.6 %fusion.81 = f32[1,16,8,1024]{3,2,1,0:T(8,128)S(1)} fusion(f32[16,8,1024]{2,1,0:T(8,128)S(1)} %fusion.4, f32[2,16,256,1024]{3,2,1,0:T(8,128)} %param.4, f32[2,16,8,1,256]{4,2,1,3,0:T(8,128)S(1)} %bitcast.234), kind=kOutput, calls=%fused_computation.63 | convolution fusion | flops 402784256 | bytes 17956864 | tf_op jit(solution)/shard_map/fvr,frs->fvs/dot_general | solution.py:27
  249.7 11.5 %fusion.75 = f32[1,16,8,1024]{3,2,1,0:T(8,128)S(1)} fusion(f32[16,8,1024]{2,1,0:T(8,128)S(1)} %fusion.6, f32[2,16,256,1024]{3,2,1,0:T(8,128)} %param.4, f32[2,16,8,1,256]{4,2,1,3,0:T(8,128)S(1)} %bitcast.235), kind=kOutput, calls=%fused_computation.61 | convolution fusion | flops 402784256 | bytes 17956864 | tf_op jit(solution)/shard_map/fvr,frs->fvs/dot_general | solution.py:22
  262.4 24.1 %reduce-scatter.9.cloned.1.call-done = f32[2,16,8,256]{3,2,1,0:T(8,128)} async-done(((f32[2,16,8,1024]{3,2,1,0:T(8,128)}), f32[2,16,8,256]{3,2,1,0:T(8,128)}) %reduce-scatter.9.cloned.1.call-update) | async-done | bytes 262160 | tf_op jit(solution)/shard_map/reduce_scatter | solution.py:38
  287.5 10.4 %all_to_all.124 = f32[2,16,8,256]{3,1,0,2:T(8,128)S(1)} all-to-all(f32[2,16,8,256]{3,1,0,2:T(8,128)S(1)} %copy.52), channel_id=1, replica_groups=mesh['freq'=8,'rcv'=4] {'freq'}, dimensions={2} | all-to-all | bytes 524288 | tf_op jit(solution)/shard_map/all_to_all | solution.py:48
  299.5 9.5 %all_to_all.125 = f32[2,128,1,256]{3,0,2,1:T(2,128)S(1)} all-to-all(f32[2,128,1,256]{3,0,2,1:T(2,128)S(1)} %copy.55), channel_id=1, replica_groups=mesh['freq'=8,'rcv'=4] {'freq'}, dimensions={1} | all-to-all | bytes 524288 | tf_op jit(solution)/shard_map/all_to_all | solution.py:44
  309.2 11.5 %fusion.105 = f32[16,8,1024]{2,1,0:T(8,128)S(1)} fusion(f32[2,16,256,1024]{3,2,1,0:T(8,128)} %param.4, f32[2,16,8,1,256]{4,2,1,3,0:T(8,128)S(1)} %bitcast.236), kind=kOutput, calls=%fused_computation.71 | convolution fusion | flops 402784256 | bytes 17432576 | tf_op jit(solution)/shard_map/fvr,frs->fvs/dot_general | solution.py:25
  320.7 11.5 %fusion.102 = f32[16,8,1024]{2,1,0:T(8,128)S(1)} fusion(f32[2,16,256,1024]{3,2,1,0:T(8,128)} %param.4, f32[2,16,8,1,256]{4,2,1,3,0:T(8,128)S(1)} %bitcast.237), kind=kOutput, calls=%fused_computation.70 | convolution fusion | flops 402784256 | bytes 17432576 | tf_op jit(solution)/shard_map/fvr,frs->fvs/dot_general | solution.py:24
  332.1 11.7 %fusion.93 = f32[1,16,8,1024]{3,2,1,0:T(8,128)S(1)} fusion(f32[16,8,1024]{2,1,0:T(8,128)S(1)} %fusion.105, f32[2,16,256,1024]{3,2,1,0:T(8,128)} %param.4, f32[2,16,8,1,256]{4,2,1,3,0:T(8,128)S(1)} %bitcast.238), kind=kOutput, calls=%fused_computation.67 | convolution fusion | flops 402784256 | bytes 17956864 | tf_op jit(solution)/shard_map/fvr,frs->fvs/dot_general | solution.py:27
  343.9 11.5 %fusion.87 = f32[1,16,8,1024]{3,2,1,0:T(8,128)S(1)} fusion(f32[16,8,1024]{2,1,0:T(8,128)S(1)} %fusion.102, f32[2,16,256,1024]{3,2,1,0:T(8,128)} %param.4, f32[2,16,8,1,256]{4,2,1,3,0:T(8,128)S(1)} %bitcast.239), kind=kOutput, calls=%fused_computation.65 | convolution fusion | flops 402784256 | bytes 17956864 | tf_op jit(solution)/shard_map/fvr,frs->fvs/dot_general | solution.py:22
  356.4 24.1 %reduce-scatter.11.cloned.1.call-done = f32[2,16,8,256]{3,2,1,0:T(8,128)} async-done(((f32[2,16,8,1024]{3,2,1,0:T(8,128)}), f32[2,16,8,256]{3,2,1,0:T(8,128)}) %reduce-scatter.11.cloned.1.call-update) | async-done | bytes 262160 | tf_op jit(solution)/shard_map/reduce_scatter | solution.py:38
  381.6 10.4 %all_to_all.126 = f32[2,16,8,256]{3,1,0,2:T(8,128)S(1)} all-to-all(f32[2,16,8,256]{3,1,0,2:T(8,128)S(1)} %copy.58), channel_id=1, replica_groups=mesh['freq'=8,'rcv'=4] {'freq'}, dimensions={2} | all-to-all | bytes 524288 | tf_op jit(solution)/shard_map/all_to_all | solution.py:48
  (43 shorter events, 14.9 us)
Async XLA Ops:
  7.2 90.0 %reduce-scatter.5.cloned.1.call-start = ((), (), s32[]{:S(2)}) async-start(), calls=%async_computation.12 | async-start | bytes 1310720 | tf_op jit(solution)/shard_map/reduce_scatter | solution.py:38
  22.9 79.7 %copy-start.3 = (s32[128]{0:T(128)S(1)}, s32[128]{0:T(128)}, u32[]{:S(2)}) copy-start(s32[128]{0:T(128)} %param.7) | copy-start | bytes 1540
  22.9 86.6 %copy-start.2 = (s32[1,256]{1,0:T(1,128)S(1)}, s32[1,256]{1,0:T(1,128)}, u32[]{:S(2)}) copy-start(s32[1,256]{1,0:T(1,128)} %param.6) | copy-start | bytes 3076
  98.9 10.6 %all-to-all-start.1 = ((f32[2,16,8,256]{3,1,0,2:T(8,128)}), f32[2,16,8,256]{3,1,0,2:T(8,128)S(1)}, u32[]{:S(2)}, u32[]{:S(2)}) async-start(f32[2,16,8,256]{3,1,0,2:T(8,128)} %copy.40), calls=%async_computation.2 | async-start | bytes 524288 | tf_op jit(solution)/shard_map/all_to_all | solution.py:48
  102.6 89.6 %reduce-scatter.7.cloned.1.call-start = ((), (), s32[]{:S(2)}) async-start(), calls=%async_computation.13 | async-start | bytes 1310720 | tf_op jit(solution)/shard_map/reduce_scatter | solution.py:38
  120.8 82.9 %copy-start = (f32[1,256,512]{2,1,0:T(8,128)S(1)}, f32[1,256,512]{2,1,0:T(8,128)}, u32[]{:S(2)}) copy-start(f32[1,256,512]{2,1,0:T(8,128)} %param.5) | copy-start | bytes 1572868
  168.1 118.4 %reduce-scatter.9.cloned.1.call-start = ((), (), s32[]{:S(2)}) async-start(), calls=%async_computation.14 | async-start | bytes 1310720 | tf_op jit(solution)/shard_map/reduce_scatter | solution.py:38
  262.3 118.3 %reduce-scatter.11.cloned.1.call-start = ((), (), s32[]{:S(2)}) async-start(), calls=%async_computation.15 | async-start | bytes 1310720 | tf_op jit(solution)/shard_map/reduce_scatter | solution.py:38
  298.6 56.7 %copy-start.1 = (f32[256,512]{1,0:T(8,128)}, f32[256,512]{1,0:T(8,128)S(1)}, u32[]{:S(2)}) copy-start(f32[256,512]{1,0:T(8,128)S(1)} %fusion.114) | copy-start | bytes 1572868
Sparse Core Ops, SparseCore 0:
  70.5 26.6 reduce-scatter.4
  168.2 23.9 reduce-scatter.6
  262.4 23.9 reduce-scatter.8
  356.6 23.9 reduce-scatter.10
where the time goes:
time: 409 us; the launch traced here: 401 us
  matrix products  192 us (47%)
  waiting for transfers between devices  106 us (26%)
  blocking collectives  71.7 us (18%)
  between operations  14.4 us (4%)
  local copies, waits for them, and re-layouts  6.39 us (2%)
  other arithmetic  6.08 us (1%)
    reduce_scatter x4, waiting for transfers between devices, multiply(): lax.psum_scatter(partial_terms, 'rcv', scatter_dimension=3, tiled=True)  99.1 us
    dot_general x4, matrix products, complex_product(): jnp.einsum(form, left[1], right[0], precision=lax.Precision.HIGHEST)  47 us
    dot_general x4, matrix products, complex_product(): jnp.einsum(form, left[0], right[1], precision=lax.Precision.HIGHEST)  46 us
    dot_general x4, matrix products, complex_product(): jnp.einsum(form, left[0], right[0], precision=lax.Precision.HIGHEST)  45.9 us
    dot_general x4, matrix products, complex_product(): jnp.einsum(form, left[1], right[1], precision=lax.Precision.HIGHEST)  45.9 us
    all_to_all x4, blocking collectives, convolve(): lax.all_to_all(spectral_field, 'freq', split_axis=1, concat_axis=2, tiled...  40.6 us
    all_to_all x3, blocking collectives, convolve(): lax.all_to_all(kernel_product, 'freq', split_axis=2, concat_axis=1, tiled...  31.1 us
  transfers between devices with their start and end apart: 5, of which 5 were waited for; matrix products, arithmetic and copies ran while one was open for 0% of the time, Pallas kernels for 0%

commit v1 on v0

v1 whole, which is shorter than its diff:
```python
import functools
import math

import jax
import jax.numpy as jnp
from jax import lax
from jax.experimental import pallas as pl
from jax.experimental.pallas import tpu as pltpu
from jax.sharding import PartitionSpec as P

ITERS = 2
F32, BF16 = jnp.float32, jnp.bfloat16
VMEM = pl.BlockSpec(memory_space=pltpu.VMEM)
ANY = pl.BlockSpec(memory_space=pl.ANY)


def call(body, ins, outs, args, mib, scratch=(), alias=None, flops=0):
    return pl.pallas_call(
        body,
        in_specs=ins,
        out_specs=tuple(VMEM for _ in outs),
        out_shape=tuple(outs),
        scratch_shapes=scratch,
        input_output_aliases=alias or {},
        compiler_params=pltpu.CompilerParams(vmem_limit_bytes=mib << 20),
    )(*args)


def halves(x):
    high = x.astype(BF16)
    return high, (x - high.astype(F32)).astype(BF16)


def dot(a, b, left, right):
    return lax.dot_general(a, b, (((left,), (right,)), ((), ())), preferred_element_type=F32)


def dot3(a, b, left, right):
    return (
        dot(a[0], b[0], left, right) + dot(a[0], b[1], left, right) + dot(a[1], b[0], left, right)
    )


def spectrum_body(table, x, th, tl, out):
    t = halves(table[...])
    th[...] = t[0]
    tl[...] = t[1]
    out[...] = dot3(t, halves(x[...]), 1, 1)


def mute_body(last, add, keep, scale, onset, product, th, tl, *rest):
    rest = list(rest)
    base = rest.pop(0) if add else None
    table = (th[...], tl[...])
    y = dot3(halves((product[...] * scale[...]).T), table, 1, 0)
    t = lax.broadcasted_iota(jnp.int32, y.shape, 1)
    y = jnp.where(t < onset[...], y, 0.0)
    if last:
        rest.pop(0)[...] = base[...] + y if add else y
        return
    if keep:
        rest.pop(0)[...] = y
    s = dot3(table, halves(y), 1, 1)
    rest.pop(0)[...] = s + base[...] if add else s


def hold_body(blocks, kernel, place, high, low, buf, sem):
    n = kernel.shape[1]
    rows = kernel.shape[2]

    def copy(k, slot):
        return pltpu.make_async_copy(kernel.at[:, k], buf.at[slot], sem.at[slot])

    copy(0, 0).start()

    @pl.loop(0, n)
    def _(k):
        slot = lax.rem(k, 2)

        @pl.when(k + 1 < n)
        def _():
            copy(k + 1, 1 - slot).start()

        copy(k, slot).wait()
        for b in range(blocks):
            col = pl.multiple_of(jnp.bitwise_xor(place[0], b) * rows, rows)
            for c in range(2):
                x = buf[slot, c, :, pl.ds(col, rows)]
                h, l = halves(x if b == 0 else x.T)
                high[c, k, pl.ds(b * rows, rows), :] = h
                low[c, k, pl.ds(b * rows, rows), :] = l


def product_body(parity, blocks, first, high, low, *rest):
    fields = rest[: len(blocks)]
    total, out = (None, rest[-1]) if first else (rest[-2], rest[-1])
    _, n, v, rows = out.shape

    def one(k, carry):
        parts = [None, None]
        for b, x in zip(blocks, fields):
            field = jnp.concatenate([x[0, k], x[1, k]], axis=0)
            h, l = halves(field)
            both = jnp.concatenate([h, l], axis=0)
            for c in range(2):
                p = dot(both, high[c, k, pl.ds(b * rows, rows), :], 1, 0)
                p = p[: 2 * v] + p[2 * v :] + dot(h, low[c, k, pl.ds(b * rows, rows), :], 1, 0)
                parts[c] = p if parts[c] is None else parts[c] + p
        re = parts[0][:v] - parity * parts[1][v:]
        im = parity * parts[1][:v] + parts[0][v:]
        out[0, k] = re if first else total[0, k] + re
        out[1, k] = im if first else total[1, k] + im
        return carry

    lax.fori_loop(0, n, one, 0, unroll=2 if n % 2 == 0 else 1)


def body(z_size, groups, kernel, focus_start, onset, freq_order):
    sds = jax.ShapeDtypeStruct
    _, n, rows, receivers = kernel.shape
    own, samples = focus_start.shape[0], focus_start.shape[2]
    n_f = freq_order.shape[0] // n
    points = n_f * own
    place = lax.axis_index("rcv")[None].astype(jnp.int32)

    order = jnp.broadcast_to(freq_order.reshape(n_f, 1, n), (n_f, 2, n)).reshape(-1)
    part = jnp.broadcast_to(jnp.arange(2).reshape(1, 2, 1), (n_f, 2, n)).reshape(-1)
    phase = order[:, None] * jnp.arange(samples, dtype=jnp.int32)[None, :] % samples
    angle = 2.0 * math.pi / samples * phase.astype(F32)
    table = jnp.where(part[:, None] == 0, jnp.cos(angle), -jnp.sin(angle))
    scale = (jnp.where(order == 0, 1.0, 2.0).astype(F32) / samples)[:, None]
    n_rows = 2 * freq_order.shape[0]

    traces = focus_start.reshape(own * rows, samples)
    limit = onset.reshape(own * rows, 1)
    th, tl, start = call(
        spectrum_body,
        [VMEM] * 2,
        [sds((n_rows, samples), BF16)] * 2 + [sds((n_rows, own * rows), F32)],
        (table, traces),
        16,
    )

    held = None

    def product(spectrum, parity):
        nonlocal held
        s = spectrum.reshape(n_f, 2 * n, own, rows)
        x = lax.all_to_all(s, "freq", split_axis=0, concat_axis=0, tiled=True)
        x = x.reshape(n_f, 2, n, own, rows).transpose(1, 2, 0, 3, 4).reshape(2, n, points, rows)
        far = [x] + [
            lax.ppermute(x, "rcv", [(i, i ^ d) for i in range(z_size)]) for d in range(1, z_size)
        ]
        if held is None:
            shape = (2, n, receivers, rows)
            held = pl.pallas_call(
                functools.partial(hold_body, z_size),
                in_specs=[ANY, pl.BlockSpec(memory_space=pltpu.SMEM)],
                out_specs=(VMEM, VMEM),
                out_shape=(pltpu.VMEM(shape, BF16), pltpu.VMEM(shape, BF16)),
                scratch_shapes=[
                    pltpu.VMEM((2, 2, rows, receivers), F32),
                    pltpu.SemaphoreType.DMA((2,)),
                ],
                compiler_params=pltpu.CompilerParams(vmem_limit_bytes=16 << 20),
            )(kernel, place)
        total = None
        for blocks in groups:
            args = (*held, *[far[b] for b in blocks])
            first = total is None
            if not first:
                args = (*args, total)
            (total,) = call(
                functools.partial(product_body, parity, blocks, first),
                [VMEM] * len(args),
                [sds((2, n, points, rows), F32)],
                args,
                12,
                alias=None if first else {len(args) - 1: 0},
            )
        back = total.reshape(2 * n, n_f, own, rows).transpose(1, 0, 2, 3)
        back = lax.all_to_all(back, "freq", split_axis=0, concat_axis=0, tiled=True)
        return back.reshape(n_rows, own * rows)

    def mute(back, last, add, keep):
        outs = [sds((own * rows, samples), F32)] if last or keep else []
        outs += [] if last else [sds((n_rows, own * rows), F32)]
        args = (scale, limit, back, th, tl)
        if add:
            args = (*args, traces if last else start)
        got = call(
            functools.partial(mute_body, last, add, keep), [VMEM] * len(args), outs, args, 16
        )
        return got

    field = start
    for iteration in range(ITERS):
        final = iteration == ITERS - 1
        got = mute(product(field, 1.0), False, False, final)
        downgoing, field = got if final else (None, got[0])
        got = mute(product(field, -1.0), final, True, False)
        field = got[0]
    return field.reshape(focus_start.shape), downgoing.reshape(focus_start.shape)


def solution(mesh):
    in_specs = (P(None, "freq", "rcv", None), P("freq", "rcv", None), P("freq", "rcv"), P())
    out_specs = (P("freq", "rcv", None), P("freq", "rcv", None))
    z_size = mesh.shape["rcv"]
    groups = [[b] for b in range(z_size)]
    return jax.shard_map(
        functools.partial(body, z_size, groups),
        mesh=mesh,
        in_specs=in_specs,
        out_specs=out_specs,
        check_vma=False,
    )
```

time: 409 us -> 224 us (0.55); the launches traced: 401 us -> 223 us
  matrix products: 192 us -> 0 us
  waiting for transfers between devices: 106 us -> 38 us
  Pallas kernels: 0 us -> 59 us
  local copies, waits for them, and re-layouts: 6.39 us -> 33.1 us
  starting transfers between devices: 3.82 us -> 21.6 us
  between operations: 14.4 us -> 0.88 us
    dot_general x24 -> x0, matrix products: 192 us -> none  [the longest x4 47 us: complex_product(): jnp.einsum(form, left[1], right[0], precision=lax.Precision.HIGHEST)]
    reduce_scatter x4 -> x0, waiting for transfers between devices: 99.1 us -> none  [multiply(): lax.psum_scatter(partial_terms, 'rcv', scatter_dimension=3, tiled=True)]
    pallas_call x0 -> x22, Pallas kernels: none -> 59 us  [the longest x21 40 us: call(): pl.pallas_call(body, in_specs=ins, out_specs=tuple((VMEM for _ in outs)),...]
    ppermute x0 -> x12, waiting for transfers between devices: none -> 31.5 us  [product(): lax.ppermute(x, 'rcv', [(i, i ^ d) for i in range(z_size)])]
    unnamed x8 -> x24, local copies, waits for them, and re-layouts: 0.03 us -> 30.2 us
    ppermute x0 -> x12, starting transfers between devices: none -> 18.2 us  [product(): lax.ppermute(x, 'rcv', [(i, i ^ d) for i in range(z_size)])]
    reduce_scatter x4 -> x0, local copies, waits for them, and re-layouts: 4.85 us -> none  [multiply(): lax.psum_scatter(partial_terms, 'rcv', scatter_dimension=3, tiled=True)]
    another operation x4 -> x0, other arithmetic: 4.31 us -> none  [complex_product(): return jnp.stack([real_part, imag_part])]
  transfers between devices with their start and end apart: 5 -> 13, of which waited for: 5 -> 6; matrix products, arithmetic and copies ran while one was open for 0% -> 0% of each run, Pallas kernels for 0% -> 20%
where the time goes in v1:
time: 224 us; the launch traced here: 223 us
  blocking collectives  67.9 us (30%)
  Pallas kernels  59 us (26%)
  waiting for transfers between devices  38 us (17%)
  local copies, waits for them, and re-layouts  33.1 us (15%)
  starting transfers between devices  21.6 us (10%)
    pallas_call x21, Pallas kernels, call(): pl.pallas_call(body, in_specs=ins, out_specs=tuple((VMEM for _ in outs)),...  40 us
    all_to_all x4, blocking collectives, product(): x = lax.all_to_all(s, 'freq', split_axis=0, concat_axis=0, tiled=True)  39.8 us
    ppermute x12, waiting for transfers between devices, product(): lax.ppermute(x, 'rcv', [(i, i ^ d) for i in range(z_size)])  31.5 us
    unnamed x24, local copies, waits for them, and re-layouts  30.2 us
    all_to_all x3, blocking collectives, product(): back = lax.all_to_all(back, 'freq', split_axis=0, concat_axis=0, tiled=True)  28.1 us
    pallas_call x1, Pallas kernels, product(): pl.pallas_call(functools.partial(hold_body, z_size), in_specs=[ANY, pl.Bl...  19 us
    ppermute x12, starting transfers between devices, product(): lax.ppermute(x, 'rcv', [(i, i ^ d) for i in range(z_size)])  18.2 us
    all_to_all x1, waiting for transfers between devices, product(): back = lax.all_to_all(back, 'freq', split_axis=0, concat_axis=0, tiled=True)  6.55 us
  transfers between devices with their start and end apart: 13, of which 6 were waited for; matrix products, arithmetic and copies ran while one was open for 0% of the time, Pallas kernels for 20%

profile of v1, /device:TPU:0, one launch (start us, length us, event | category | flops | bytes accessed | tf_op | source)
XLA Modules:
  0.0 222.7 jit_solution(2128943806005330262)
XLA Ops:
  1.6 2.2 negate_select_fusion.2.table
  5.2 11.9 %all_to_all.40 = f32[8,32,1,256]{3,1,2,0:T(8,128)S(1)} all-to-all(f32[8,32,1,256]{3,1,2,0:T(8,128)S(1)} %bitcast.83), channel_id=1, replica_groups=mesh['freq'=8,'rcv'=4] {'freq'}, dimensions={0} | all-to-all | bytes 524288 | tf_op jit(solution)/shard_map/all_to_all | solution.py:149
  18.9 2.6 %collective-permute-start.1 = (f32[2,16,8,256]{3,2,1,0:T(8,128)S(1)}, f32[2,16,8,256]{3,2,1,0:T(8,128)S(1)}, u32[]{:S(2)}, u32[]{:S(2)}) collective-permute-start(f32[2,16,8,256]{3,2,1,0:T(8,128)S(1)} %bitcast.66), channel_id=1, source_target_pairs={{0,2},{1,3},{2,0},{3,1},{4,6},{5,7},{6,4},{7,5},{8,10},{9,11},{10,... | collective-permute-start | bytes 786440 | tf_op jit(solution)/shard_map/ppermute | solution.py:152
  21.7 19.0 %shard_map.59 = (bf16[2,16,1024,256]{3,2,1,0:T(8,128)(2,1)S(1)}, bf16[2,16,1024,256]{3,2,1,0:T(8,128)(2,1)S(1)}) custom-call(f32[2,16,256,1024]{3,2,1,0:T(8,128)} %kernel.1, s32[1]{0:T(128)} %bitcast.1.place), custom_call_target="tpu_custom_call" | custom-call | tf_op jit(solution)/shard_map/pallas_call | solution.py:156
  40.7 5.7 %copy-done = bf16[2,16,1024,256]{3,2,1,0:T(8,128)(2,1)} copy-done((bf16[2,16,1024,256]{3,2,1,0:T(8,128)(2,1)}, bf16[2,16,1024,256]{3,2,1,0:T(8,128)(2,1)S(1)}, u32[]{:S(2)}) %copy-start) | copy-done | bytes 16777240
  46.5 11.8 %copy-done.1 = bf16[2,16,1024,256]{3,2,1,0:T(8,128)(2,1)S(1)} copy-done((bf16[2,16,1024,256]{3,2,1,0:T(8,128)(2,1)S(1)}, bf16[2,16,1024,256]{3,2,1,0:T(8,128)(2,1)}, u32[]{:S(2)}) %copy-start.1) | copy-done | bytes 16777240
  60.4 2.2 shard_map.62.rest_1_
  62.6 2.2 shard_map.63.rest_1_
  67.8 3.4 %all-to-all-start.1 = ((f32[8,32,1,256]{3,1,2,0:T(8,128)}), f32[8,32,1,256]{3,1,2,0:T(8,128)S(1)}, u32[]{:S(2)}, u32[]{:S(2)}) async-start(f32[8,32,1,256]{3,1,2,0:T(8,128)} %bitcast.56), calls=%async_computation.1 | async-start | bytes 524288 | tf_op jit(solution)/shard_map/all_to_all | solution.py:182
  71.5 6.6 %all-to-all-done.1 = f32[8,32,1,256]{3,1,2,0:T(8,128)S(1)} async-done(((f32[8,32,1,256]{3,1,2,0:T(8,128)}), f32[8,32,1,256]{3,1,2,0:T(8,128)S(1)}, u32[]{:S(2)}, u32[]{:S(2)}) %all-to-all-start.1) | async-done | bytes 262176 | tf_op jit(solution)/shard_map/all_to_all | solution.py:182
  79.1 9.3 %all_to_all.41 = f32[8,32,1,256]{3,1,2,0:T(8,128)S(1)} all-to-all(f32[8,32,1,256]{3,1,2,0:T(8,128)S(1)} %bitcast.82), channel_id=1, replica_groups=mesh['freq'=8,'rcv'=4] {'freq'}, dimensions={0} | all-to-all | bytes 524288 | tf_op jit(solution)/shard_map/all_to_all | solution.py:149
  89.3 3.5 %collective-permute-start.4 = (f32[2,16,8,256]{3,2,1,0:T(8,128)S(1)}, f32[2,16,8,256]{3,2,1,0:T(8,128)S(1)}, u32[]{:S(2)}, u32[]{:S(2)}) collective-permute-start(f32[2,16,8,256]{3,2,1,0:T(8,128)S(1)} %bitcast.70), channel_id=1, source_target_pairs={{0,2},{1,3},{2,0},{3,1},{4,6},{5,7},{6,4},{7,5},{8,10},{9,11},{10,... | collective-permute-start | bytes 786440 | tf_op jit(solution)/shard_map/ppermute | solution.py:152
  93.0 5.8 %copy-done.2 = bf16[2,16,1024,256]{3,2,1,0:T(8,128)(2,1)S(1)} copy-done((bf16[2,16,1024,256]{3,2,1,0:T(8,128)(2,1)S(1)}, bf16[2,16,1024,256]{3,2,1,0:T(8,128)(2,1)}, u32[]{:S(2)}) %copy-start.2) | copy-done | bytes 16777240
  98.8 5.8 %copy-done.4 = bf16[2,16,1024,256]{3,2,1,0:T(8,128)(2,1)S(1)} copy-done((bf16[2,16,1024,256]{3,2,1,0:T(8,128)(2,1)S(1)}, bf16[2,16,1024,256]{3,2,1,0:T(8,128)(2,1)}, u32[]{:S(2)}) %copy-start.4) | copy-done | bytes 16777240
  106.7 2.2 shard_map.67.rest_1_
  108.9 2.3 %collective-permute-done.4.rest_0_ = f32[2,16,8,256]{3,2,1,0:T(8,128)S(1)} collective-permute-done((f32[2,16,8,256]{3,2,1,0:T(8,128)S(1)}, f32[2,16,8,256]{3,2,1,0:T(8,128)S(1)}, u32[]{:S(2)}, u32[]{:S(2)}) %collective-permute-start.4) | collective-permute-done | bytes 262176 | tf_op jit(solution)/shard_map/ppermute | solution.py:152
  111.2 2.2 shard_map.68.rest_1_
  113.4 2.2 shard_map.69
  115.7 9.4 %all_to_all.42 = f32[8,32,1,256]{3,1,2,0:T(8,128)S(1)} all-to-all(f32[8,32,1,256]{3,1,2,0:T(8,128)S(1)} %bitcast.89), channel_id=1, replica_groups=mesh['freq'=8,'rcv'=4] {'freq'}, dimensions={0} | all-to-all | bytes 524288 | tf_op jit(solution)/shard_map/all_to_all | solution.py:182
  126.2 9.3 %all_to_all.43 = f32[8,32,1,256]{3,1,2,0:T(8,128)S(1)} all-to-all(f32[8,32,1,256]{3,1,2,0:T(8,128)S(1)} %bitcast.86), channel_id=1, replica_groups=mesh['freq'=8,'rcv'=4] {'freq'}, dimensions={0} | all-to-all | bytes 524288 | tf_op jit(solution)/shard_map/all_to_all | solution.py:149
  135.7 2.3 %collective-permute-start.8 = (f32[2,16,8,256]{3,2,1,0:T(8,128)S(1)}, f32[2,16,8,256]{3,2,1,0:T(8,128)S(1)}, u32[]{:S(2)}, u32[]{:S(2)}) collective-permute-start(f32[2,16,8,256]{3,2,1,0:T(8,128)S(1)} %bitcast.73), channel_id=1, source_target_pairs={{0,1},{1,0},{2,3},{3,2},{4,5},{5,4},{6,7},{7,6},{8,9},{9,8},{10,11... | collective-permute-start | bytes 786440 | tf_op jit(solution)/shard_map/ppermute | solution.py:152
  142.6 5.7 %collective-permute-done.8.rest_0_ = f32[2,16,8,256]{3,2,1,0:T(8,128)S(1)} collective-permute-done((f32[2,16,8,256]{3,2,1,0:T(8,128)S(1)}, f32[2,16,8,256]{3,2,1,0:T(8,128)S(1)}, u32[]{:S(2)}, u32[]{:S(2)}) %collective-permute-start.8) | collective-permute-done | bytes 262176 | tf_op jit(solution)/shard_map/ppermute | solution.py:152
  150.5 8.8 %collective-permute-done.7.rest_0_ = f32[2,16,8,256]{3,2,1,0:T(8,128)S(1)} collective-permute-done((f32[2,16,8,256]{3,2,1,0:T(8,128)S(1)}, f32[2,16,8,256]{3,2,1,0:T(8,128)S(1)}, u32[]{:S(2)}, u32[]{:S(2)}) %collective-permute-start.7) | collective-permute-done | bytes 262176 | tf_op jit(solution)/shard_map/ppermute | solution.py:152
  161.5 2.2 shard_map.74
  163.7 9.3 %all_to_all.44 = f32[8,32,1,256]{3,1,2,0:T(8,128)S(1)} all-to-all(f32[8,32,1,256]{3,1,2,0:T(8,128)S(1)} %bitcast.90), channel_id=1, replica_groups=mesh['freq'=8,'rcv'=4] {'freq'}, dimensions={0} | all-to-all | bytes 524288 | tf_op jit(solution)/shard_map/all_to_all | solution.py:182
  174.7 9.3 %all_to_all.45 = f32[8,32,1,256]{3,1,2,0:T(8,128)S(1)} all-to-all(f32[8,32,1,256]{3,1,2,0:T(8,128)S(1)} %bitcast.88), channel_id=1, replica_groups=mesh['freq'=8,'rcv'=4] {'freq'}, dimensions={0} | all-to-all | bytes 524288 | tf_op jit(solution)/shard_map/all_to_all | solution.py:149
  190.9 5.7 %collective-permute-done.11.rest_0_ = f32[2,16,8,256]{3,2,1,0:T(8,128)S(1)} collective-permute-done((f32[2,16,8,256]{3,2,1,0:T(8,128)S(1)}, f32[2,16,8,256]{3,2,1,0:T(8,128)S(1)}, u32[]{:S(2)}, u32[]{:S(2)}) %collective-permute-start.11) | collective-permute-done | bytes 262176 | tf_op jit(solution)/shard_map/ppermute | solution.py:152
  196.7 2.2 shard_map.77.rest_1_
  198.8 8.8 %collective-permute-done.10.rest_0_ = f32[2,16,8,256]{3,2,1,0:T(8,128)S(1)} collective-permute-done((f32[2,16,8,256]{3,2,1,0:T(8,128)S(1)}, f32[2,16,8,256]{3,2,1,0:T(8,128)S(1)}, u32[]{:S(2)}, u32[]{:S(2)}) %collective-permute-start.10) | collective-permute-done | bytes 262176 | tf_op jit(solution)/shard_map/ppermute | solution.py:152
  207.7 2.2 shard_map.78.rest_1_
  209.9 2.2 shard_map.79
  212.1 9.3 %all_to_all.46 = f32[8,32,1,256]{3,1,2,0:T(8,128)S(1)} all-to-all(f32[8,32,1,256]{3,1,2,0:T(8,128)S(1)} %bitcast.91), channel_id=1, replica_groups=mesh['freq'=8,'rcv'=4] {'freq'}, dimensions={0} | all-to-all | bytes 524288 | tf_op jit(solution)/shard_map/all_to_all | solution.py:182
  (66 shorter events, 34.4 us)
Async XLA Ops:
  3.8 1.0 copy-start.5
  17.3 43.1 %collective-permute-start.2 = (f32[2,16,8,256]{3,2,1,0:T(8,128)S(1)}, f32[2,16,8,256]{3,2,1,0:T(8,128)S(1)}, u32[]{:S(2)}, u32[]{:S(2)}) collective-permute-start(f32[2,16,8,256]{3,2,1,0:T(8,128)S(1)} %bitcast.65), channel_id=1, source_target_pairs={{0,1},{1,0},{2,3},{3,2},{4,5},{5,4},{6,7},{7,6},{8,9},{9,8},{10,11... | collective-permute-start | bytes 786440 | tf_op jit(solution)/shard_map/ppermute | solution.py:152
  18.9 43.7 %collective-permute-start.1 = (f32[2,16,8,256]{3,2,1,0:T(8,128)S(1)}, f32[2,16,8,256]{3,2,1,0:T(8,128)S(1)}, u32[]{:S(2)}, u32[]{:S(2)}) collective-permute-start(f32[2,16,8,256]{3,2,1,0:T(8,128)S(1)} %bitcast.66), channel_id=1, source_target_pairs={{0,2},{1,3},{2,0},{3,1},{4,6},{5,7},{6,4},{7,5},{8,10},{9,11},{10,... | collective-permute-start | bytes 786440 | tf_op jit(solution)/shard_map/ppermute | solution.py:152
  21.5 43.3 %collective-permute-start = (f32[2,16,8,256]{3,2,1,0:T(8,128)S(1)}, f32[2,16,8,256]{3,2,1,0:T(8,128)S(1)}, u32[]{:S(2)}, u32[]{:S(2)}) collective-permute-start(f32[2,16,8,256]{3,2,1,0:T(8,128)S(1)} %bitcast.67), channel_id=1, source_target_pairs={{0,3},{1,2},{2,1},{3,0},{4,7},{5,6},{6,5},{7,4},{8,11},{9,10},{10,... | collective-permute-start | bytes 786440 | tf_op jit(solution)/shard_map/ppermute | solution.py:152
  40.7 5.7 %copy-start = (bf16[2,16,1024,256]{3,2,1,0:T(8,128)(2,1)}, bf16[2,16,1024,256]{3,2,1,0:T(8,128)(2,1)S(1)}, u32[]{:S(2)}) copy-start(bf16[2,16,1024,256]{3,2,1,0:T(8,128)(2,1)S(1)} %get-tuple-element.9.high) | copy-start | bytes 50331652
  46.5 18.3 %copy-start.3 = (bf16[2,16,1024,256]{3,2,1,0:T(8,128)(2,1)}, bf16[2,16,1024,256]{3,2,1,0:T(8,128)(2,1)S(1)}, u32[]{:S(2)}) copy-start(bf16[2,16,1024,256]{3,2,1,0:T(8,128)(2,1)S(1)} %get-tuple-element.10.low) | copy-start | bytes 50331652
  46.5 11.8 %copy-start.1 = (bf16[2,16,1024,256]{3,2,1,0:T(8,128)(2,1)S(1)}, bf16[2,16,1024,256]{3,2,1,0:T(8,128)(2,1)}, u32[]{:S(2)}) copy-start(bf16[2,16,1024,256]{3,2,1,0:T(8,128)(2,1)} %copy-done) | copy-start | bytes 50331652
  64.8 6.5 %copy-start.7 = (s32[1,256]{1,0:T(1,128)S(1)}, s32[1,256]{1,0:T(1,128)}, u32[]{:S(2)}) copy-start(s32[1,256]{1,0:T(1,128)} %param.6) | copy-start | bytes 3076
  67.8 10.3 %all-to-all-start.1 = ((f32[8,32,1,256]{3,1,2,0:T(8,128)}), f32[8,32,1,256]{3,1,2,0:T(8,128)S(1)}, u32[]{:S(2)}, u32[]{:S(2)}) async-start(f32[8,32,1,256]{3,1,2,0:T(8,128)} %bitcast.56), calls=%async_computation.1 | async-start | bytes 524288 | tf_op jit(solution)/shard_map/all_to_all | solution.py:182
  88.6 18.1 %collective-permute-start.5 = (f32[2,16,8,256]{3,2,1,0:T(8,128)S(1)}, f32[2,16,8,256]{3,2,1,0:T(8,128)S(1)}, u32[]{:S(2)}, u32[]{:S(2)}) collective-permute-start(f32[2,16,8,256]{3,2,1,0:T(8,128)S(1)} %bitcast.69), channel_id=1, source_target_pairs={{0,1},{1,0},{2,3},{3,2},{4,5},{5,4},{6,7},{7,6},{8,9},{9,8},{10,11... | collective-permute-start | bytes 786440 | tf_op jit(solution)/shard_map/ppermute | solution.py:152
  89.3 21.9 %collective-permute-start.4 = (f32[2,16,8,256]{3,2,1,0:T(8,128)S(1)}, f32[2,16,8,256]{3,2,1,0:T(8,128)S(1)}, u32[]{:S(2)}, u32[]{:S(2)}) collective-permute-start(f32[2,16,8,256]{3,2,1,0:T(8,128)S(1)} %bitcast.70), channel_id=1, source_target_pairs={{0,2},{1,3},{2,0},{3,1},{4,6},{5,7},{6,4},{7,5},{8,10},{9,11},{10,... | collective-permute-start | bytes 786440 | tf_op jit(solution)/shard_map/ppermute | solution.py:152
  92.8 20.6 %collective-permute-start.3 = (f32[2,16,8,256]{3,2,1,0:T(8,128)S(1)}, f32[2,16,8,256]{3,2,1,0:T(8,128)S(1)}, u32[]{:S(2)}, u32[]{:S(2)}) collective-permute-start(f32[2,16,8,256]{3,2,1,0:T(8,128)S(1)} %bitcast.71), channel_id=1, source_target_pairs={{0,3},{1,2},{2,1},{3,0},{4,7},{5,6},{6,5},{7,4},{8,11},{9,10},{10,... | collective-permute-start | bytes 786440 | tf_op jit(solution)/shard_map/ppermute | solution.py:152
  93.0 5.8 %copy-start.2 = (bf16[2,16,1024,256]{3,2,1,0:T(8,128)(2,1)S(1)}, bf16[2,16,1024,256]{3,2,1,0:T(8,128)(2,1)}, u32[]{:S(2)}) copy-start(bf16[2,16,1024,256]{3,2,1,0:T(8,128)(2,1)} %copy-done) | copy-start | bytes 50331652
  98.8 5.8 %copy-start.4 = (bf16[2,16,1024,256]{3,2,1,0:T(8,128)(2,1)S(1)}, bf16[2,16,1024,256]{3,2,1,0:T(8,128)(2,1)}, u32[]{:S(2)}) copy-start(bf16[2,16,1024,256]{3,2,1,0:T(8,128)(2,1)} %copy-done.3) | copy-start | bytes 50331652
  111.2 29.2 %slice-start = ((s8[16777216]{0:T(1024)(128)(4,1)}), s8[4194304]{0:T(1024)(128)(4,1)S(1)}, s32[]{:S(2)}) async-start(s8[16777216]{0:T(1024)(128)(4,1)} %bitcast.57), calls=%async_computation.8 | async-start | bytes 8388608
  111.2 29.2 %slice-start.1 = ((s8[16777216]{0:T(1024)(128)(4,1)}), s8[4194304]{0:T(1024)(128)(4,1)S(1)}, s32[]{:S(2)}) async-start(s8[16777216]{0:T(1024)(128)(4,1)} %bitcast.57), calls=%async_computation.9 | async-start | bytes 8388608
  113.4 27.0 %slice-start.2 = ((s8[16777216]{0:T(1024)(128)(4,1)}), s8[4194304]{0:T(1024)(128)(4,1)S(1)}, s32[]{:S(2)}) async-start(s8[16777216]{0:T(1024)(128)(4,1)} %bitcast.57), calls=%async_computation.10 | async-start | bytes 8388608
  113.4 27.0 %slice-start.3 = ((s8[16777216]{0:T(1024)(128)(4,1)}), s8[4194304]{0:T(1024)(128)(4,1)S(1)}, s32[]{:S(2)}) async-start(s8[16777216]{0:T(1024)(128)(4,1)} %bitcast.57), calls=%async_computation.11 | async-start | bytes 8388608
  135.7 12.6 %collective-permute-start.8 = (f32[2,16,8,256]{3,2,1,0:T(8,128)S(1)}, f32[2,16,8,256]{3,2,1,0:T(8,128)S(1)}, u32[]{:S(2)}, u32[]{:S(2)}) collective-permute-start(f32[2,16,8,256]{3,2,1,0:T(8,128)S(1)} %bitcast.73), channel_id=1, source_target_pairs={{0,1},{1,0},{2,3},{3,2},{4,5},{5,4},{6,7},{7,6},{8,9},{9,8},{10,11... | collective-permute-start | bytes 786440 | tf_op jit(solution)/shard_map/ppermute | solution.py:152
  138.0 21.3 %collective-permute-start.7 = (f32[2,16,8,256]{3,2,1,0:T(8,128)S(1)}, f32[2,16,8,256]{3,2,1,0:T(8,128)S(1)}, u32[]{:S(2)}, u32[]{:S(2)}) collective-permute-start(f32[2,16,8,256]{3,2,1,0:T(8,128)S(1)} %bitcast.74), channel_id=1, source_target_pairs={{0,2},{1,3},{2,0},{3,1},{4,6},{5,7},{6,4},{7,5},{8,10},{9,11},{10,... | collective-permute-start | bytes 786440 | tf_op jit(solution)/shard_map/ppermute | solution.py:152
  139.0 22.4 %collective-permute-start.6 = (f32[2,16,8,256]{3,2,1,0:T(8,128)S(1)}, f32[2,16,8,256]{3,2,1,0:T(8,128)S(1)}, u32[]{:S(2)}, u32[]{:S(2)}) collective-permute-start(f32[2,16,8,256]{3,2,1,0:T(8,128)S(1)} %bitcast.75), channel_id=1, source_target_pairs={{0,3},{1,2},{2,1},{3,0},{4,7},{5,6},{6,5},{7,4},{8,11},{9,10},{10,... | collective-permute-start | bytes 786440 | tf_op jit(solution)/shard_map/ppermute | solution.py:152
  184.2 12.5 %collective-permute-start.11 = (f32[2,16,8,256]{3,2,1,0:T(8,128)S(1)}, f32[2,16,8,256]{3,2,1,0:T(8,128)S(1)}, u32[]{:S(2)}, u32[]{:S(2)}) collective-permute-start(f32[2,16,8,256]{3,2,1,0:T(8,128)S(1)} %bitcast.77), channel_id=1, source_target_pairs={{0,1},{1,0},{2,3},{3,2},{4,5},{5,4},{6,7},{7,6},{8,9},{9,8},{10,11... | collective-permute-start | bytes 786440 | tf_op jit(solution)/shard_map/ppermute | solution.py:152
  186.4 21.3 %collective-permute-start.10 = (f32[2,16,8,256]{3,2,1,0:T(8,128)S(1)}, f32[2,16,8,256]{3,2,1,0:T(8,128)S(1)}, u32[]{:S(2)}, u32[]{:S(2)}) collective-permute-start(f32[2,16,8,256]{3,2,1,0:T(8,128)S(1)} %bitcast.78), channel_id=1, source_target_pairs={{0,2},{1,3},{2,0},{3,1},{4,6},{5,7},{6,4},{7,5},{8,10},{9,11},{10,... | collective-permute-start | bytes 786440 | tf_op jit(solution)/shard_map/ppermute | solution.py:152
  187.4 22.4 %collective-permute-start.9 = (f32[2,16,8,256]{3,2,1,0:T(8,128)S(1)}, f32[2,16,8,256]{3,2,1,0:T(8,128)S(1)}, u32[]{:S(2)}, u32[]{:S(2)}) collective-permute-start(f32[2,16,8,256]{3,2,1,0:T(8,128)S(1)} %bitcast.79), channel_id=1, source_target_pairs={{0,3},{1,2},{2,1},{3,0},{4,7},{5,6},{6,5},{7,4},{8,11},{9,10},{10,... | collective-permute-start | bytes 786440 | tf_op jit(solution)/shard_map/ppermute | solution.py:152
  209.8 11.6 %copy-start.6 = (f32[1,256,512]{2,1,0:T(8,128)S(1)}, f32[1,256,512]{2,1,0:T(8,128)}, u32[]{:S(2)}) copy-start(f32[1,256,512]{2,1,0:T(8,128)} %param.5) | copy-start | bytes 1572868

commit v2 on v1

v2 whole, which is shorter than its diff:
```python
import functools
import math

import jax
import jax.numpy as jnp
from jax import lax
from jax.experimental import pallas as pl
from jax.experimental.pallas import tpu as pltpu
from jax.sharding import PartitionSpec as P

ITERS = 2
F32, BF16 = jnp.float32, jnp.bfloat16
VMEM = pl.BlockSpec(memory_space=pltpu.VMEM)
ANY = pl.BlockSpec(memory_space=pl.ANY)


def call(body, ins, outs, args, mib, alias=None):
    return pl.pallas_call(
        body,
        in_specs=ins,
        out_specs=tuple(VMEM for _ in outs),
        out_shape=tuple(outs),
        input_output_aliases=alias or {},
        compiler_params=pltpu.CompilerParams(vmem_limit_bytes=mib << 20),
    )(*args)


def halves(x):
    high = x.astype(BF16)
    return high, (x - high.astype(F32)).astype(BF16)


def dot(a, b, left, right):
    return lax.dot_general(a, b, (((left,), (right,)), ((), ())), preferred_element_type=F32)


def dot3(a, b, left, right):
    return (
        dot(a[0], b[0], left, right) + dot(a[0], b[1], left, right) + dot(a[1], b[0], left, right)
    )


def column(row, length, stride):
    shape = (length, row.shape[1])
    hit = lax.broadcasted_iota(jnp.int32, shape, 0) // stride
    hit = hit == lax.broadcasted_iota(jnp.int32, shape, 1)
    return jnp.sum(jnp.where(hit, row.astype(F32), 0.0), axis=1, keepdims=True)


def spectrum_body(order, onset, x, th, tl, scale, limit, out):
    rows, samples = th.shape
    q = column(order[...], rows, 2)
    scale[...] = jnp.where(q == 0.0, 1.0, 2.0) / samples
    limit[...] = column(onset[...], limit.shape[0], 1).astype(jnp.int32)
    part = lax.broadcasted_iota(jnp.int32, (rows, samples), 0) & 1
    time = lax.broadcasted_iota(jnp.int32, (rows, samples), 1)
    phase = lax.rem(q.astype(jnp.int32) * time + part * (samples // 4), samples)
    table = halves(jnp.cos(2.0 * math.pi / samples * phase.astype(F32)))
    th[...] = table[0]
    tl[...] = table[1]
    out[...] = dot3(table, halves(x[...]), 1, 1)


def mute_body(last, add, keep, scale, onset, product, th, tl, *rest):
    rest = list(rest)
    base = rest.pop(0) if add else None
    table = (th[...], tl[...])
    y = dot3(halves((product[...] * scale[...]).T), table, 1, 0)
    t = lax.broadcasted_iota(jnp.int32, y.shape, 1)
    y = jnp.where(t < onset[...], y, 0.0)
    if last:
        rest.pop(0)[...] = base[...] + y if add else y
        return
    if keep:
        rest.pop(0)[...] = y
    s = dot3(table, halves(y), 1, 1)
    rest.pop(0)[...] = s + base[...] if add else s


def hold_body(blocks, kernel, place, *rest):
    *outs, buf, sem = rest
    n = kernel.shape[1]
    rows = kernel.shape[2]

    def copy(k, slot):
        return pltpu.make_async_copy(kernel.at[:, k], buf.at[slot], sem.at[slot])

    copy(0, 0).start()

    @pl.loop(0, n)
    def _(k):
        slot = lax.rem(k, 2)

        @pl.when(k + 1 < n)
        def _():
            copy(k + 1, 1 - slot).start()

        copy(k, slot).wait()
        for b in range(blocks):
            col = pl.multiple_of(jnp.bitwise_xor(place[0], b) * rows, rows)
            for c in range(2):
                x = buf[slot, c, :, pl.ds(col, rows)]
                h, l = halves(x if b == 0 else x.T)
                outs[2 * b][c, k] = h
                outs[2 * b + 1][c, k] = l


def product_body(parity, pieces, first, *rest):
    highs, lows = rest[: len(pieces)], rest[len(pieces) : 2 * len(pieces)]
    fields = rest[2 * len(pieces) : 3 * len(pieces)]
    total, out = (None, rest[-1]) if first else (rest[-2], rest[-1])
    v, rows = out.shape[2:]
    spans = sorted({(at, at + x.shape[0]) for (_, at), x in zip(pieces, fields)})
    cuts = sorted({end for span in spans for end in span})

    def one(k, here):
        parts = [None, None]
        for high, low, at, x in here:
            h, l = halves(x[k - at].reshape(2 * v, rows))
            both = jnp.concatenate([h, l], axis=0)
            for c in range(2):
                p = dot(both, high[c, k], 1, 0)
                p = p[: 2 * v] + p[2 * v :] + dot(h, low[c, k], 1, 0)
                parts[c] = p if parts[c] is None else parts[c] + p
        re = parts[0][:v] - parity * parts[1][v:]
        im = parity * parts[1][:v] + parts[0][v:]
        out[k, 0] = re if first else total[k, 0] + re
        out[k, 1] = im if first else total[k, 1] + im

    for begin, end in zip(cuts[:-1], cuts[1:]):
        here = [
            (high, low, at, x)
            for (_, at), high, low, x in zip(pieces, highs, lows, fields)
            if at <= begin and end <= at + x.shape[0]
        ]
        if not here:
            continue
        step = math.gcd(end - begin, max(1, 8 // len(here)))

        @pl.loop(begin // step, end // step)
        def _(i):
            for j in range(step):
                one(i * step + j, here)


def body(z_size, kernel, focus_start, onset, freq_order):
    sds = jax.ShapeDtypeStruct
    _, n, rows, receivers = kernel.shape
    own, samples = focus_start.shape[0], focus_start.shape[2]
    n_f = freq_order.shape[0] // n
    points = n_f * own
    place = lax.axis_index("rcv")[None].astype(jnp.int32)

    n_rows = 2 * freq_order.shape[0]
    traces = focus_start.reshape(own * rows, samples)
    th, tl, scale, limit, start = call(
        spectrum_body,
        [VMEM] * 3,
        [sds((n_rows, samples), BF16)] * 2
        + [sds((n_rows, 1), F32), sds((own * rows, 1), jnp.int32), sds((n_rows, own * rows), F32)],
        (freq_order.reshape(1, -1), onset.reshape(1, -1), traces),
        8,
    )

    held = None

    def shift(x, d):
        return lax.ppermute(x, "rcv", [(i, i ^ d) for i in range(z_size)])

    def gather(x):
        half = n // 2
        if z_size != 4 or n % 2:
            return [[(d, 0, shift(x, d) if d else x)] for d in range(z_size)]
        low, high = x[:half], x[half:]
        b0 = shift(low, 2)
        c1 = shift(high, 3)
        b1 = shift(high, 2)
        a = shift(x, 1)
        c0 = shift(b0, 1)
        return [[(0, 0, x)], [(2, 0, b0), (3, half, c1)], [(2, half, b1), (1, 0, a)], [(3, 0, c0)]]

    def product(spectrum, parity):
        nonlocal held
        s = spectrum.reshape(n_f, 2 * n, own, rows)
        x = lax.all_to_all(s, "freq", split_axis=0, concat_axis=0, tiled=True)
        x = x.reshape(n_f, n, 2, own, rows).transpose(1, 2, 0, 3, 4).reshape(n, 2, points, rows)
        groups = gather(x)
        if held is None:
            shape = (2, n, rows, rows)
            held = pl.pallas_call(
                functools.partial(hold_body, z_size),
                in_specs=[ANY, pl.BlockSpec(memory_space=pltpu.SMEM)],
                out_specs=(VMEM,) * (2 * z_size),
                out_shape=(pltpu.VMEM(shape, BF16),) * (2 * z_size),
                scratch_shapes=[
                    pltpu.VMEM((2, 2, rows, receivers), F32),
                    pltpu.SemaphoreType.DMA((2,)),
                ],
                compiler_params=pltpu.CompilerParams(vmem_limit_bytes=9 << 20),
            )(kernel, place)
        total = None
        for group in groups:
            args = [held[2 * b + h] for h in (0, 1) for b, _, _ in group]
            args += [field for _, _, field in group]
            first = total is None
            if not first:
                args.append(total)
            (total,) = call(
                functools.partial(product_body, parity, [piece[:2] for piece in group], first),
                [VMEM] * len(args),
                [sds((n, 2, points, rows), F32)],
                args,
                8,
                alias=None if first else {len(args) - 1: 0},
            )
        back = total.reshape(2 * n, n_f, own, rows).transpose(1, 0, 2, 3)
        back = lax.all_to_all(back, "freq", split_axis=0, concat_axis=0, tiled=True)
        return back.reshape(n_rows, own * rows)

    def mute(back, last, add, keep):
        outs = [sds((own * rows, samples), F32)] if last or keep else []
        outs += [] if last else [sds((n_rows, own * rows), F32)]
        args = (scale, limit, back, th, tl)
        if add:
            args = (*args, traces if last else start)
        got = call(
            functools.partial(mute_body, last, add, keep), [VMEM] * len(args), outs, args, 8
        )
        return got

    field = start
    for iteration in range(ITERS):
        final = iteration == ITERS - 1
        got = mute(product(field, 1.0), False, False, final)
        downgoing, field = got if final else (None, got[0])
        got = mute(product(field, -1.0), final, True, False)
        field = got[0]
    return field.reshape(focus_start.shape), downgoing.reshape(focus_start.shape)


def solution(mesh):
    in_specs = (P(None, "freq", "rcv", None), P("freq", "rcv", None), P("freq", "rcv"), P())
    out_specs = (P("freq", "rcv", None), P("freq", "rcv", None))
    z_size = mesh.shape["rcv"]
    return jax.shard_map(
        functools.partial(body, z_size),
        mesh=mesh,
        in_specs=in_specs,
        out_specs=out_specs,
        check_vma=False,
    )
```

time: 224 us -> 200 us (0.89)
  local copies, waits for them, and re-layouts: 33.1 us -> 3.47 us
  starting transfers between devices: 21.6 us -> 45.6 us
  waiting for transfers between devices: 38 us -> 23.7 us
  Pallas kernels: 59 us -> 49 us
  blocking collectives: 67.9 us -> 77.1 us
    unnamed x24 -> x8, local copies, waits for them, and re-layouts: 30.2 us -> 2.38 us
    ppermute x12 -> x20, starting transfers between devices: 18.2 us -> 45.6 us  [shift(): return lax.ppermute(x, 'rcv', [(i, i ^ d) for i in range(z_size)])]
    pallas_call x21, Pallas kernels: 40 us -> 30 us  [call(): pl.pallas_call(body, in_specs=ins, out_specs=tuple((VMEM for _ in outs)),...]
    all_to_all x3 -> x4, blocking collectives: 28.1 us -> 37.3 us  [product(): back = lax.all_to_all(back, 'freq', split_axis=0, concat_axis=0, tiled=True)]
    ppermute x12 -> x20, waiting for transfers between devices: 31.5 us -> 23.7 us  [shift(): return lax.ppermute(x, 'rcv', [(i, i ^ d) for i in range(z_size)])]
    all_to_all x1 -> x0, waiting for transfers between devices: 6.55 us -> none  [product(): back = lax.all_to_all(back, 'freq', split_axis=0, concat_axis=0, tiled=True)]
    all_to_all x1 -> x0, starting transfers between devices: 3.41 us -> none  [product(): back = lax.all_to_all(back, 'freq', split_axis=0, concat_axis=0, tiled=True)]
  transfers between devices with their start and end apart: 13 -> 20, of which waited for: 6 -> 8; matrix products, arithmetic and copies ran while one was open for 0% -> 0% of each run, Pallas kernels for 20% -> 19%
where the time goes in v2:
time: 200 us
  blocking collectives  77.1 us (39%)
  Pallas kernels  49 us (24%)
  starting transfers between devices  45.6 us (23%)
  waiting for transfers between devices  23.7 us (12%)
  local copies, waits for them, and re-layouts  3.47 us (2%)
    ppermute x20, starting transfers between devices, shift(): return lax.ppermute(x, 'rcv', [(i, i ^ d) for i in range(z_size)])  45.6 us
    all_to_all x4, blocking collectives, product(): x = lax.all_to_all(s, 'freq', split_axis=0, concat_axis=0, tiled=True)  39.8 us
    all_to_all x4, blocking collectives, product(): back = lax.all_to_all(back, 'freq', split_axis=0, concat_axis=0, tiled=True)  37.3 us
    pallas_call x21, Pallas kernels, call(): pl.pallas_call(body, in_specs=ins, out_specs=tuple((VMEM for _ in outs)),...  30 us
    ppermute x20, waiting for transfers between devices, shift(): return lax.ppermute(x, 'rcv', [(i, i ^ d) for i in range(z_size)])  23.7 us
    pallas_call x1, Pallas kernels, product(): pl.pallas_call(functools.partial(hold_body, z_size), in_specs=[ANY, pl.Bl...  19 us
  transfers between devices with their start and end apart: 20, of which 8 were waited for; matrix products, arithmetic and copies ran while one was open for 0% of the time, Pallas kernels for 19%

profile of v2, /device:TPU:0, one launch (start us, length us, event | category | flops | bytes accessed | tf_op | source)
XLA Modules:
  0.0 199.7 jit_solution(659576256529828681)
XLA Ops:
  3.0 2.3 %shard_map.59 = (bf16[256,512]{1,0:T(8,128)(2,1)S(1)}, bf16[256,512]{1,0:T(8,128)(2,1)S(1)}, f32[256,1]{1,0:T(8,128)S(1)}, s32[256,1]{1,0:T(8,128)S(1)}, f32[256,256]{1,0:T(8,128)S(1)}) custom-call(s32[1,128]{1,0:T(1,128)S(1)} %bitcast.99, s32[1,256]{1,0:T(1,128)S(1)} %copy-done.2, f32[256,512]{1,0:T(8,128)S(1)} %bitcast.89), custom_call_target="tpu_custom_call" | custom-call | tf_op jit(solution)/shard_map/pallas_call | solution.py:18
  5.3 11.9 %all_to_all.40 = f32[8,32,1,256]{3,1,2,0:T(8,128)S(1)} all-to-all(f32[8,32,1,256]{3,1,2,0:T(8,128)S(1)} %bitcast.93), channel_id=1, replica_groups=mesh['freq'=8,'rcv'=4] {'freq'}, dimensions={0} | all-to-all | bytes 524288 | tf_op jit(solution)/shard_map/all_to_all | solution.py:185
  17.4 1.6 collective-permute-start.3
  19.0 2.7 %collective-permute-start = (f32[8,2,8,256]{3,2,1,0:T(8,128)S(1)}, f32[8,2,8,256]{3,2,1,0:T(8,128)S(1)}, u32[]{:S(2)}, u32[]{:S(2)}) collective-permute-start(f32[8,2,8,256]{3,2,1,0:T(8,128)S(1)} %get-tuple-element.39), channel_id=1, source_target_pairs={{0,2},{1,3},{2,0},{3,1},{4,6},{5,7},{6,4},{7,5},{8,10},{9,11},{10,... | collective-permute-start | bytes 393224 | tf_op jit(solution)/shard_map/ppermute | solution.py:168
  21.9 1.7 collective-permute-start.2
  23.6 5.0 %collective-permute-done.rest_4_ = f32[8,2,8,256]{3,2,1,0:T(8,128)S(1)} collective-permute-done((f32[8,2,8,256]{3,2,1,0:T(8,128)S(1)}, f32[8,2,8,256]{3,2,1,0:T(8,128)S(1)}, u32[]{:S(2)}, u32[]{:S(2)}) %collective-permute-start) | collective-permute-done | bytes 131104 | tf_op jit(solution)/shard_map/ppermute | solution.py:168
  28.6 4.2 %collective-permute-start.1 = (f32[8,2,8,256]{3,2,1,0:T(8,128)S(1)}, f32[8,2,8,256]{3,2,1,0:T(8,128)S(1)}, u32[]{:S(2)}, u32[]{:S(2)}) collective-permute-start(f32[8,2,8,256]{3,2,1,0:T(8,128)S(1)} %collective-permute-done.rest_4_), channel_id=1, source_target_pairs={{0,1},{1,0},{2,3},{3,2},{4,5},{5,4},{6,7},{7,6},{8,9},{9,8},{10,11... | collective-permute-start | bytes 393224 | tf_op jit(solution)/shard_map/ppermute | solution.py:168
  32.8 19.0 %shard_map.60 = (bf16[2,16,256,256]{3,2,1,0:T(8,128)(2,1)S(1)}, bf16[2,16,256,256]{3,2,1,0:T(8,128)(2,1)S(1)}, bf16[2,16,256,256]{3,2,1,0:T(8,128)(2,1)S(1)}, bf...) custom-call(f32[2,16,256,1024]{3,2,1,0:T(8,128)} %kernel.1, ...), custom_call_target="tpu_custom_call" | custom-call | tf_op jit(solution)/shard_map/pallas_call | solution.py:190
  54.5 2.2 %shard_map.63.rest_3_ = f32[16,2,8,256]{3,2,1,0:T(8,128)S(1)} custom-call(bf16[2,16,256,256]{3,2,1,0:T(8,128)(2,1)S(1)} %get-tuple-element.22.rest_0_, bf16[2,16,256,256]{3,2,1,0:T(8,128)(2,1)S(1)} %get-tuple-element.23.rest_1_, bf16[2,16,256,256]{3,2,1,0:T(8,128)(2,1)S(1)} %get-tuple-element.24.rest_2_, ...), custom_call_target="tpu_custom_call", output_to_operand_aliasing={{}: (6, {})} | custom-call | tf_op jit(solution)/shard_map/pallas_call | solution.py:18
  57.5 9.3 %all_to_all.41 = f32[8,32,1,256]{3,1,2,0:T(8,128)S(1)} all-to-all(f32[8,32,1,256]{3,1,2,0:T(8,128)S(1)} %bitcast.100), channel_id=1, replica_groups=mesh['freq'=8,'rcv'=4] {'freq'}, dimensions={0} | all-to-all | bytes 524288 | tf_op jit(solution)/shard_map/all_to_all | solution.py:217
  68.0 9.3 %all_to_all.42 = f32[8,32,1,256]{3,1,2,0:T(8,128)S(1)} all-to-all(f32[8,32,1,256]{3,1,2,0:T(8,128)S(1)} %bitcast.92), channel_id=1, replica_groups=mesh['freq'=8,'rcv'=4] {'freq'}, dimensions={0} | all-to-all | bytes 524288 | tf_op jit(solution)/shard_map/all_to_all | solution.py:185
  77.5 3.9 %collective-permute-start.5 = (f32[8,2,8,256]{3,2,1,0:T(8,128)S(1)}, f32[8,2,8,256]{3,2,1,0:T(8,128)S(1)}, u32[]{:S(2)}, u32[]{:S(2)}) collective-permute-start(f32[8,2,8,256]{3,2,1,0:T(8,128)S(1)} %get-tuple-element.37), channel_id=1, source_target_pairs={{0,2},{1,3},{2,0},{3,1},{4,6},{5,7},{6,4},{7,5},{8,10},{9,11},{10,... | collective-permute-start | bytes 393224 | tf_op jit(solution)/shard_map/ppermute | solution.py:168
  82.9 2.0 %collective-permute-start.7 = (f32[8,2,8,256]{3,2,1,0:T(8,128)S(1)}, f32[8,2,8,256]{3,2,1,0:T(8,128)S(1)}, u32[]{:S(2)}, u32[]{:S(2)}) collective-permute-start(f32[8,2,8,256]{3,2,1,0:T(8,128)S(1)} %get-tuple-element.36), channel_id=1, source_target_pairs={{0,2},{1,3},{2,0},{3,1},{4,6},{5,7},{6,4},{7,5},{8,10},{9,11},{10,... | collective-permute-start | bytes 393224 | tf_op jit(solution)/shard_map/ppermute | solution.py:168
  84.9 2.2 %collective-permute-done.5.rest_4_ = f32[8,2,8,256]{3,2,1,0:T(8,128)S(1)} collective-permute-done((f32[8,2,8,256]{3,2,1,0:T(8,128)S(1)}, f32[8,2,8,256]{3,2,1,0:T(8,128)S(1)}, u32[]{:S(2)}, u32[]{:S(2)}) %collective-permute-start.5) | collective-permute-done | bytes 131104 | tf_op jit(solution)/shard_map/ppermute | solution.py:168
  87.1 7.8 %collective-permute-start.6 = (f32[8,2,8,256]{3,2,1,0:T(8,128)S(1)}, f32[8,2,8,256]{3,2,1,0:T(8,128)S(1)}, u32[]{:S(2)}, u32[]{:S(2)}) collective-permute-start(f32[8,2,8,256]{3,2,1,0:T(8,128)S(1)} %collective-permute-done.5.rest_4_), channel_id=1, source_target_pairs={{0,1},{1,0},{2,3},{3,2},{4,5},{5,4},{6,7},{7,6},{8,9},{9,8},{10,11... | collective-permute-start | bytes 393224 | tf_op jit(solution)/shard_map/ppermute | solution.py:168
  98.6 2.2 %shard_map.68.rest_3_ = f32[16,2,8,256]{3,2,1,0:T(8,128)S(1)} custom-call(bf16[2,16,256,256]{3,2,1,0:T(8,128)(2,1)S(1)} %get-tuple-element.22.rest_0_, bf16[2,16,256,256]{3,2,1,0:T(8,128)(2,1)S(1)} %get-tuple-element.23.rest_1_, bf16[2,16,256,256]{3,2,1,0:T(8,128)(2,1)S(1)} %get-tuple-element.24.rest_2_, ...), custom_call_target="tpu_custom_call", output_to_operand_aliasing={{}: (6, {})} | custom-call | tf_op jit(solution)/shard_map/pallas_call | solution.py:18
  101.6 9.3 %all_to_all.43 = f32[8,32,1,256]{3,1,2,0:T(8,128)S(1)} all-to-all(f32[8,32,1,256]{3,1,2,0:T(8,128)S(1)} %bitcast.101), channel_id=1, replica_groups=mesh['freq'=8,'rcv'=4] {'freq'}, dimensions={0} | all-to-all | bytes 524288 | tf_op jit(solution)/shard_map/all_to_all | solution.py:217
  112.0 9.3 %all_to_all.44 = f32[8,32,1,256]{3,1,2,0:T(8,128)S(1)} all-to-all(f32[8,32,1,256]{3,1,2,0:T(8,128)S(1)} %bitcast.96), channel_id=1, replica_groups=mesh['freq'=8,'rcv'=4] {'freq'}, dimensions={0} | all-to-all | bytes 524288 | tf_op jit(solution)/shard_map/all_to_all | solution.py:185
  122.4 3.5 %collective-permute-start.10 = (f32[8,2,8,256]{3,2,1,0:T(8,128)S(1)}, f32[8,2,8,256]{3,2,1,0:T(8,128)S(1)}, u32[]{:S(2)}, u32[]{:S(2)}) collective-permute-start(f32[8,2,8,256]{3,2,1,0:T(8,128)S(1)} %get-tuple-element.35), channel_id=1, source_target_pairs={{0,2},{1,3},{2,0},{3,1},{4,6},{5,7},{6,4},{7,5},{8,10},{9,11},{10,... | collective-permute-start | bytes 393224 | tf_op jit(solution)/shard_map/ppermute | solution.py:168
  127.6 4.4 %collective-permute-done.10.rest_4_ = f32[8,2,8,256]{3,2,1,0:T(8,128)S(1)} collective-permute-done((f32[8,2,8,256]{3,2,1,0:T(8,128)S(1)}, f32[8,2,8,256]{3,2,1,0:T(8,128)S(1)}, u32[]{:S(2)}, u32[]{:S(2)}) %collective-permute-start.10) | collective-permute-done | bytes 131104 | tf_op jit(solution)/shard_map/ppermute | solution.py:168
  131.9 5.4 %collective-permute-start.11 = (f32[8,2,8,256]{3,2,1,0:T(8,128)S(1)}, f32[8,2,8,256]{3,2,1,0:T(8,128)S(1)}, u32[]{:S(2)}, u32[]{:S(2)}) collective-permute-start(f32[8,2,8,256]{3,2,1,0:T(8,128)S(1)} %collective-permute-done.10.rest_4_), channel_id=1, source_target_pairs={{0,1},{1,0},{2,3},{3,2},{4,5},{5,4},{6,7},{7,6},{8,9},{9,8},{10,11... | collective-permute-start | bytes 393224 | tf_op jit(solution)/shard_map/ppermute | solution.py:168
  140.1 2.5 %collective-permute-done.12.rest_4_ = f32[8,2,8,256]{3,2,1,0:T(8,128)S(1)} collective-permute-done((f32[8,2,8,256]{3,2,1,0:T(8,128)S(1)}, f32[8,2,8,256]{3,2,1,0:T(8,128)S(1)}, u32[]{:S(2)}, u32[]{:S(2)}) %collective-permute-start.12) | collective-permute-done | bytes 131104 | tf_op jit(solution)/shard_map/ppermute | solution.py:168
  142.6 2.2 %shard_map.73.rest_3_ = f32[16,2,8,256]{3,2,1,0:T(8,128)S(1)} custom-call(bf16[2,16,256,256]{3,2,1,0:T(8,128)(2,1)S(1)} %get-tuple-element.22.rest_0_, bf16[2,16,256,256]{3,2,1,0:T(8,128)(2,1)S(1)} %get-tuple-element.23.rest_1_, bf16[2,16,256,256]{3,2,1,0:T(8,128)(2,1)S(1)} %get-tuple-element.24.rest_2_, ...), custom_call_target="tpu_custom_call", output_to_operand_aliasing={{}: (6, {})} | custom-call | tf_op jit(solution)/shard_map/pallas_call | solution.py:18
  145.6 9.3 %all_to_all.45 = f32[8,32,1,256]{3,1,2,0:T(8,128)S(1)} all-to-all(f32[8,32,1,256]{3,1,2,0:T(8,128)S(1)} %bitcast.102), channel_id=1, replica_groups=mesh['freq'=8,'rcv'=4] {'freq'}, dimensions={0} | all-to-all | bytes 524288 | tf_op jit(solution)/shard_map/all_to_all | solution.py:217
  154.9 1.7 shard_map.75
  156.6 9.3 %all_to_all.46 = f32[8,32,1,256]{3,1,2,0:T(8,128)S(1)} all-to-all(f32[8,32,1,256]{3,1,2,0:T(8,128)S(1)} %bitcast.98), channel_id=1, replica_groups=mesh['freq'=8,'rcv'=4] {'freq'}, dimensions={0} | all-to-all | bytes 524288 | tf_op jit(solution)/shard_map/all_to_all | solution.py:185
  166.7 2.5 %collective-permute-start.15 = (f32[8,2,8,256]{3,2,1,0:T(8,128)S(1)}, f32[8,2,8,256]{3,2,1,0:T(8,128)S(1)}, u32[]{:S(2)}, u32[]{:S(2)}) collective-permute-start(f32[8,2,8,256]{3,2,1,0:T(8,128)S(1)} %get-tuple-element.33), channel_id=1, source_target_pairs={{0,2},{1,3},{2,0},{3,1},{4,6},{5,7},{6,4},{7,5},{8,10},{9,11},{10,... | collective-permute-start | bytes 393224 | tf_op jit(solution)/shard_map/ppermute | solution.py:168
  171.1 5.1 %collective-permute-done.15.rest_4_ = f32[8,2,8,256]{3,2,1,0:T(8,128)S(1)} collective-permute-done((f32[8,2,8,256]{3,2,1,0:T(8,128)S(1)}, f32[8,2,8,256]{3,2,1,0:T(8,128)S(1)}, u32[]{:S(2)}, u32[]{:S(2)}) %collective-permute-start.15) | collective-permute-done | bytes 131104 | tf_op jit(solution)/shard_map/ppermute | solution.py:168
  176.2 3.5 %collective-permute-start.16 = (f32[8,2,8,256]{3,2,1,0:T(8,128)S(1)}, f32[8,2,8,256]{3,2,1,0:T(8,128)S(1)}, u32[]{:S(2)}, u32[]{:S(2)}) collective-permute-start(f32[8,2,8,256]{3,2,1,0:T(8,128)S(1)} %collective-permute-done.15.rest_4_), channel_id=1, source_target_pairs={{0,1},{1,0},{2,3},{3,2},{4,5},{5,4},{6,7},{7,6},{8,9},{9,8},{10,11... | collective-permute-start | bytes 393224 | tf_op jit(solution)/shard_map/ppermute | solution.py:168
  183.2 2.8 %collective-permute-done.17.rest_4_ = f32[8,2,8,256]{3,2,1,0:T(8,128)S(1)} collective-permute-done((f32[8,2,8,256]{3,2,1,0:T(8,128)S(1)}, f32[8,2,8,256]{3,2,1,0:T(8,128)S(1)}, u32[]{:S(2)}, u32[]{:S(2)}) %collective-permute-start.17) | collective-permute-done | bytes 131104 | tf_op jit(solution)/shard_map/ppermute | solution.py:168
  186.1 2.2 %shard_map.78.rest_3_ = f32[16,2,8,256]{3,2,1,0:T(8,128)S(1)} custom-call(bf16[2,16,256,256]{3,2,1,0:T(8,128)(2,1)S(1)} %get-tuple-element.22.rest_0_, bf16[2,16,256,256]{3,2,1,0:T(8,128)(2,1)S(1)} %get-tuple-element.23.rest_1_, bf16[2,16,256,256]{3,2,1,0:T(8,128)(2,1)S(1)} %get-tuple-element.24.rest_2_, ...), custom_call_target="tpu_custom_call", output_to_operand_aliasing={{}: (6, {})} | custom-call | tf_op jit(solution)/shard_map/pallas_call | solution.py:18
  189.1 9.3 %all_to_all.47 = f32[8,32,1,256]{3,1,2,0:T(8,128)S(1)} all-to-all(f32[8,32,1,256]{3,1,2,0:T(8,128)S(1)} %bitcast.103), channel_id=1, replica_groups=mesh['freq'=8,'rcv'=4] {'freq'}, dimensions={0} | all-to-all | bytes 524288 | tf_op jit(solution)/shard_map/all_to_all | solution.py:217
  (58 shorter events, 29.3 us)
Async XLA Ops:
  0.6 1.0 copy-start
  1.7 0.7 copy-start.2
  2.4 0.7 copy-start.3
  17.4 37.2 %collective-permute-start.3 = (f32[16,2,8,256]{3,2,1,0:T(8,128)S(1)}, f32[16,2,8,256]{3,2,1,0:T(8,128)S(1)}, u32[]{:S(2)}, u32[]{:S(2)}) collective-permute-start(f32[16,2,8,256]{3,2,1,0:T(8,128)S(1)} %bitcast.77), channel_id=1, source_target_pairs={{0,1},{1,0},{2,3},{3,2},{4,5},{5,4},{6,7},{7,6},{8,9},{9,8},{10,11... | collective-permute-start | bytes 786440 | tf_op jit(solution)/shard_map/ppermute | solution.py:168
  19.0 9.5 %collective-permute-start = (f32[8,2,8,256]{3,2,1,0:T(8,128)S(1)}, f32[8,2,8,256]{3,2,1,0:T(8,128)S(1)}, u32[]{:S(2)}, u32[]{:S(2)}) collective-permute-start(f32[8,2,8,256]{3,2,1,0:T(8,128)S(1)} %get-tuple-element.39), channel_id=1, source_target_pairs={{0,2},{1,3},{2,0},{3,1},{4,6},{5,7},{6,4},{7,5},{8,10},{9,11},{10,... | collective-permute-start | bytes 393224 | tf_op jit(solution)/shard_map/ppermute | solution.py:168
  21.7 31.5 %collective-permute-start.4 = (f32[8,2,8,256]{3,2,1,0:T(8,128)S(1)}, f32[8,2,8,256]{3,2,1,0:T(8,128)S(1)}, u32[]{:S(2)}, u32[]{:S(2)}) collective-permute-start(f32[8,2,8,256]{3,2,1,0:T(8,128)S(1)} %get-tuple-element.38), channel_id=1, source_target_pairs={{0,3},{1,2},{2,1},{3,0},{4,7},{5,6},{6,5},{7,4},{8,11},{9,10},{10,... | collective-permute-start | bytes 393224 | tf_op jit(solution)/shard_map/ppermute | solution.py:168
  21.9 32.6 %collective-permute-start.2 = (f32[8,2,8,256]{3,2,1,0:T(8,128)S(1)}, f32[8,2,8,256]{3,2,1,0:T(8,128)S(1)}, u32[]{:S(2)}, u32[]{:S(2)}) collective-permute-start(f32[8,2,8,256]{3,2,1,0:T(8,128)S(1)} %get-tuple-element.38), channel_id=1, source_target_pairs={{0,2},{1,3},{2,0},{3,1},{4,6},{5,7},{6,4},{7,5},{8,10},{9,11},{10,... | collective-permute-start | bytes 393224 | tf_op jit(solution)/shard_map/ppermute | solution.py:168
  28.6 28.2 %collective-permute-start.1 = (f32[8,2,8,256]{3,2,1,0:T(8,128)S(1)}, f32[8,2,8,256]{3,2,1,0:T(8,128)S(1)}, u32[]{:S(2)}, u32[]{:S(2)}) collective-permute-start(f32[8,2,8,256]{3,2,1,0:T(8,128)S(1)} %collective-permute-done.rest_4_), channel_id=1, source_target_pairs={{0,1},{1,0},{2,3},{3,2},{4,5},{5,4},{6,7},{7,6},{8,9},{9,8},{10,11... | collective-permute-start | bytes 393224 | tf_op jit(solution)/shard_map/ppermute | solution.py:168
  77.5 21.1 %collective-permute-start.8 = (f32[16,2,8,256]{3,2,1,0:T(8,128)S(1)}, f32[16,2,8,256]{3,2,1,0:T(8,128)S(1)}, u32[]{:S(2)}, u32[]{:S(2)}) collective-permute-start(f32[16,2,8,256]{3,2,1,0:T(8,128)S(1)} %bitcast.84), channel_id=1, source_target_pairs={{0,1},{1,0},{2,3},{3,2},{4,5},{5,4},{6,7},{7,6},{8,9},{9,8},{10,11... | collective-permute-start | bytes 786440 | tf_op jit(solution)/shard_map/ppermute | solution.py:168
  77.5 9.5 %collective-permute-start.5 = (f32[8,2,8,256]{3,2,1,0:T(8,128)S(1)}, f32[8,2,8,256]{3,2,1,0:T(8,128)S(1)}, u32[]{:S(2)}, u32[]{:S(2)}) collective-permute-start(f32[8,2,8,256]{3,2,1,0:T(8,128)S(1)} %get-tuple-element.37), channel_id=1, source_target_pairs={{0,2},{1,3},{2,0},{3,1},{4,6},{5,7},{6,4},{7,5},{8,10},{9,11},{10,... | collective-permute-start | bytes 393224 | tf_op jit(solution)/shard_map/ppermute | solution.py:168
  81.5 14.9 %collective-permute-start.9 = (f32[8,2,8,256]{3,2,1,0:T(8,128)S(1)}, f32[8,2,8,256]{3,2,1,0:T(8,128)S(1)}, u32[]{:S(2)}, u32[]{:S(2)}) collective-permute-start(f32[8,2,8,256]{3,2,1,0:T(8,128)S(1)} %get-tuple-element.36), channel_id=1, source_target_pairs={{0,3},{1,2},{2,1},{3,0},{4,7},{5,6},{6,5},{7,4},{8,11},{9,10},{10,... | collective-permute-start | bytes 393224 | tf_op jit(solution)/shard_map/ppermute | solution.py:168
  82.9 15.7 %collective-permute-start.7 = (f32[8,2,8,256]{3,2,1,0:T(8,128)S(1)}, f32[8,2,8,256]{3,2,1,0:T(8,128)S(1)}, u32[]{:S(2)}, u32[]{:S(2)}) collective-permute-start(f32[8,2,8,256]{3,2,1,0:T(8,128)S(1)} %get-tuple-element.36), channel_id=1, source_target_pairs={{0,2},{1,3},{2,0},{3,1},{4,6},{5,7},{6,4},{7,5},{8,10},{9,11},{10,... | collective-permute-start | bytes 393224 | tf_op jit(solution)/shard_map/ppermute | solution.py:168
  87.1 13.7 %collective-permute-start.6 = (f32[8,2,8,256]{3,2,1,0:T(8,128)S(1)}, f32[8,2,8,256]{3,2,1,0:T(8,128)S(1)}, u32[]{:S(2)}, u32[]{:S(2)}) collective-permute-start(f32[8,2,8,256]{3,2,1,0:T(8,128)S(1)} %collective-permute-done.5.rest_4_), channel_id=1, source_target_pairs={{0,1},{1,0},{2,3},{3,2},{4,5},{5,4},{6,7},{7,6},{8,9},{9,8},{10,11... | collective-permute-start | bytes 393224 | tf_op jit(solution)/shard_map/ppermute | solution.py:168
  121.5 21.1 %collective-permute-start.13 = (f32[16,2,8,256]{3,2,1,0:T(8,128)S(1)}, f32[16,2,8,256]{3,2,1,0:T(8,128)S(1)}, u32[]{:S(2)}, u32[]{:S(2)}) collective-permute-start(f32[16,2,8,256]{3,2,1,0:T(8,128)S(1)} %bitcast.87), channel_id=1, source_target_pairs={{0,1},{1,0},{2,3},{3,2},{4,5},{5,4},{6,7},{7,6},{8,9},{9,8},{10,11... | collective-permute-start | bytes 786440 | tf_op jit(solution)/shard_map/ppermute | solution.py:168
  122.4 9.5 %collective-permute-start.10 = (f32[8,2,8,256]{3,2,1,0:T(8,128)S(1)}, f32[8,2,8,256]{3,2,1,0:T(8,128)S(1)}, u32[]{:S(2)}, u32[]{:S(2)}) collective-permute-start(f32[8,2,8,256]{3,2,1,0:T(8,128)S(1)} %get-tuple-element.35), channel_id=1, source_target_pairs={{0,2},{1,3},{2,0},{3,1},{4,6},{5,7},{6,4},{7,5},{8,10},{9,11},{10,... | collective-permute-start | bytes 393224 | tf_op jit(solution)/shard_map/ppermute | solution.py:168
  125.9 12.9 %collective-permute-start.14 = (f32[8,2,8,256]{3,2,1,0:T(8,128)S(1)}, f32[8,2,8,256]{3,2,1,0:T(8,128)S(1)}, u32[]{:S(2)}, u32[]{:S(2)}) collective-permute-start(f32[8,2,8,256]{3,2,1,0:T(8,128)S(1)} %get-tuple-element.34), channel_id=1, source_target_pairs={{0,3},{1,2},{2,1},{3,0},{4,7},{5,6},{6,5},{7,4},{8,11},{9,10},{10,... | collective-permute-start | bytes 393224 | tf_op jit(solution)/shard_map/ppermute | solution.py:168
  126.0 16.6 %collective-permute-start.12 = (f32[8,2,8,256]{3,2,1,0:T(8,128)S(1)}, f32[8,2,8,256]{3,2,1,0:T(8,128)S(1)}, u32[]{:S(2)}, u32[]{:S(2)}) collective-permute-start(f32[8,2,8,256]{3,2,1,0:T(8,128)S(1)} %get-tuple-element.34), channel_id=1, source_target_pairs={{0,2},{1,3},{2,0},{3,1},{4,6},{5,7},{6,4},{7,5},{8,10},{9,11},{10,... | collective-permute-start | bytes 393224 | tf_op jit(solution)/shard_map/ppermute | solution.py:168
  131.9 12.9 %collective-permute-start.11 = (f32[8,2,8,256]{3,2,1,0:T(8,128)S(1)}, f32[8,2,8,256]{3,2,1,0:T(8,128)S(1)}, u32[]{:S(2)}, u32[]{:S(2)}) collective-permute-start(f32[8,2,8,256]{3,2,1,0:T(8,128)S(1)} %collective-permute-done.10.rest_4_), channel_id=1, source_target_pairs={{0,1},{1,0},{2,3},{3,2},{4,5},{5,4},{6,7},{7,6},{8,9},{9,8},{10,11... | collective-permute-start | bytes 393224 | tf_op jit(solution)/shard_map/ppermute | solution.py:168
  166.1 20.0 %collective-permute-start.18 = (f32[16,2,8,256]{3,2,1,0:T(8,128)S(1)}, f32[16,2,8,256]{3,2,1,0:T(8,128)S(1)}, u32[]{:S(2)}, u32[]{:S(2)}) collective-permute-start(f32[16,2,8,256]{3,2,1,0:T(8,128)S(1)} %bitcast.81), channel_id=1, source_target_pairs={{0,1},{1,0},{2,3},{3,2},{4,5},{5,4},{6,7},{7,6},{8,9},{9,8},{10,11... | collective-permute-start | bytes 786440 | tf_op jit(solution)/shard_map/ppermute | solution.py:168
  166.7 9.5 %collective-permute-start.15 = (f32[8,2,8,256]{3,2,1,0:T(8,128)S(1)}, f32[8,2,8,256]{3,2,1,0:T(8,128)S(1)}, u32[]{:S(2)}, u32[]{:S(2)}) collective-permute-start(f32[8,2,8,256]{3,2,1,0:T(8,128)S(1)} %get-tuple-element.33), channel_id=1, source_target_pairs={{0,2},{1,3},{2,0},{3,1},{4,6},{5,7},{6,4},{7,5},{8,10},{9,11},{10,... | collective-permute-start | bytes 393224 | tf_op jit(solution)/shard_map/ppermute | solution.py:168
  169.2 12.7 %collective-permute-start.19 = (f32[8,2,8,256]{3,2,1,0:T(8,128)S(1)}, f32[8,2,8,256]{3,2,1,0:T(8,128)S(1)}, u32[]{:S(2)}, u32[]{:S(2)}) collective-permute-start(f32[8,2,8,256]{3,2,1,0:T(8,128)S(1)} %get-tuple-element.32), channel_id=1, source_target_pairs={{0,3},{1,2},{2,1},{3,0},{4,7},{5,6},{6,5},{7,4},{8,11},{9,10},{10,... | collective-permute-start | bytes 393224 | tf_op jit(solution)/shard_map/ppermute | solution.py:168
  170.6 15.5 %collective-permute-start.17 = (f32[8,2,8,256]{3,2,1,0:T(8,128)S(1)}, f32[8,2,8,256]{3,2,1,0:T(8,128)S(1)}, u32[]{:S(2)}, u32[]{:S(2)}) collective-permute-start(f32[8,2,8,256]{3,2,1,0:T(8,128)S(1)} %get-tuple-element.32), channel_id=1, source_target_pairs={{0,2},{1,3},{2,0},{3,1},{4,6},{5,7},{6,4},{7,5},{8,10},{9,11},{10,... | collective-permute-start | bytes 393224 | tf_op jit(solution)/shard_map/ppermute | solution.py:168
  176.2 12.0 %collective-permute-start.16 = (f32[8,2,8,256]{3,2,1,0:T(8,128)S(1)}, f32[8,2,8,256]{3,2,1,0:T(8,128)S(1)}, u32[]{:S(2)}, u32[]{:S(2)}) collective-permute-start(f32[8,2,8,256]{3,2,1,0:T(8,128)S(1)} %collective-permute-done.15.rest_4_), channel_id=1, source_target_pairs={{0,1},{1,0},{2,3},{3,2},{4,5},{5,4},{6,7},{7,6},{8,9},{9,8},{10,11... | collective-permute-start | bytes 393224 | tf_op jit(solution)/shard_map/ppermute | solution.py:168
  188.2 10.2 %copy-start.1 = (f32[1,256,512]{2,1,0:T(8,128)S(1)}, f32[1,256,512]{2,1,0:T(8,128)}, u32[]{:S(2)}) copy-start(f32[1,256,512]{2,1,0:T(8,128)} %param.5) | copy-start | bytes 1572868

commit v3 on v2

--- a/solution.py
+++ b/solution.py
@@ -8,18 +8,20 @@
 from jax.experimental.pallas import tpu as pltpu
 from jax.sharding import PartitionSpec as P
 
+
 ITERS = 2
 F32, BF16 = jnp.float32, jnp.bfloat16
 VMEM = pl.BlockSpec(memory_space=pltpu.VMEM)
-ANY = pl.BlockSpec(memory_space=pl.ANY)
-
-
-def call(body, ins, outs, args, mib, alias=None):
+HBM = pl.BlockSpec(memory_space=pltpu.HBM)
+
+
+def call(body, ins, outs, args, mib=8, alias=None, scratch=()):
     return pl.pallas_call(
         body,
         in_specs=ins,
         out_specs=tuple(VMEM for _ in outs),
         out_shape=tuple(outs),
+        scratch_shapes=scratch,
         input_output_aliases=alias or {},
         compiler_params=pltpu.CompilerParams(vmem_limit_bytes=mib << 20),
     )(*args)
@@ -47,34 +49,45 @@
     return jnp.sum(jnp.where(hit, row.astype(F32), 0.0), axis=1, keepdims=True)
 
 
-def spectrum_body(order, onset, x, th, tl, scale, limit, out):
+def cosine(turn):
+    x = (2.0 * math.pi) * (0.25 - jnp.minimum(turn, 1.0 - turn))
+    square = x * x
+    series = 0.0
+    for power in range(13, 0, -2):
+        series = series * square + (-1.0) ** (power // 2) / math.factorial(power)
+    return series * x
+
+
+def spectrum_body(order_in, onset_in, x_in, th, tl, scale, limit, out, order, onset, x, sems):
+    pairs = ((order_in, order), (onset_in, onset), (x_in, x))
+    copies = [pltpu.make_async_copy(a, b, sems.at[i]) for i, (a, b) in enumerate(pairs)]
+    for copy in copies:
+        copy.start()
     rows, samples = th.shape
+    shape = (rows, samples)
+    time = lax.broadcasted_iota(jnp.int32, shape, 1).astype(F32) / samples
+    part = (lax.broadcasted_iota(jnp.int32, shape, 0) & 1).astype(F32) * 0.25
+    copies[0].wait()
     q = column(order[...], rows, 2)
     scale[...] = jnp.where(q == 0.0, 1.0, 2.0) / samples
-    limit[...] = column(onset[...], limit.shape[0], 1).astype(jnp.int32)
-    part = lax.broadcasted_iota(jnp.int32, (rows, samples), 0) & 1
-    time = lax.broadcasted_iota(jnp.int32, (rows, samples), 1)
-    phase = lax.rem(q.astype(jnp.int32) * time + part * (samples // 4), samples)
-    table = halves(jnp.cos(2.0 * math.pi / samples * phase.astype(F32)))
+    turn = q * time + part
+    table = halves(cosine(turn - jnp.floor(turn)))
     th[...] = table[0]
     tl[...] = table[1]
+    copies[1].wait()
+    limit[...] = column(onset[...], limit.shape[0], 1).astype(jnp.int32)
+    copies[2].wait()
     out[...] = dot3(table, halves(x[...]), 1, 1)
 
 
-def mute_body(last, add, keep, scale, onset, product, th, tl, *rest):
-    rest = list(rest)
-    base = rest.pop(0) if add else None
+def mute_body(last, add, scale, onset, product, th, tl, *rest):
     table = (th[...], tl[...])
     y = dot3(halves((product[...] * scale[...]).T), table, 1, 0)
     t = lax.broadcasted_iota(jnp.int32, y.shape, 1)
     y = jnp.where(t < onset[...], y, 0.0)
-    if last:
-        rest.pop(0)[...] = base[...] + y if add else y
-        return
-    if keep:
-        rest.pop(0)[...] = y
-    s = dot3(table, halves(y), 1, 1)
-    rest.pop(0)[...] = s + base[...] if add else s
+    if not last:
+        y = dot3(table, halves(y), 1, 1)
+    rest[-1][...] = rest[0][...] + y if add else y
 
 
 def hold_body(blocks, kernel, place, *rest):
@@ -155,11 +168,16 @@
     traces = focus_start.reshape(own * rows, samples)
     th, tl, scale, limit, start = call(
         spectrum_body,
-        [VMEM] * 3,
+        [HBM] * 3,
         [sds((n_rows, samples), BF16)] * 2
         + [sds((n_rows, 1), F32), sds((own * rows, 1), jnp.int32), sds((n_rows, own * rows), F32)],
         (freq_order.reshape(1, -1), onset.reshape(1, -1), traces),
-        8,
+        scratch=[
+            pltpu.VMEM((1, n_rows // 2), jnp.int32),
+            pltpu.VMEM((1, own * rows), jnp.int32),
+            pltpu.VMEM((own * rows, samples), F32),
+            pltpu.SemaphoreType.DMA((3,)),
+        ],
     )
 
     held = None
@@ -167,10 +185,10 @@
     def shift(x, d):
         return lax.ppermute(x, "rcv", [(i, i ^ d) for i in range(z_size)])
 
-    def gather(x):
+    def gather(x, relay):
         half = n // 2
-        if z_size != 4 or n % 2:
-            return [[(d, 0, shift(x, d) if d else x)] for d in range(z_size)]
+        if z_size != 4 or n % 2 or not relay:
+            return [[(0, 0, x)]] + [[(d, 0, shift(x, d))] for d in range(1, z_size)]
         low, high = x[:half], x[half:]
         b0 = shift(low, 2)
         c1 = shift(high, 3)
@@ -184,12 +202,12 @@
         s = spectrum.reshape(n_f, 2 * n, own, rows)
         x = lax.all_to_all(s, "freq", split_axis=0, concat_axis=0, tiled=True)
         x = x.reshape(n_f, n, 2, own, rows).transpose(1, 2, 0, 3, 4).reshape(n, 2, points, rows)
-        groups = gather(x)
+        groups = gather(x, held is not None)
         if held is None:
             shape = (2, n, rows, rows)
             held = pl.pallas_call(
                 functools.partial(hold_body, z_size),
-                in_specs=[ANY, pl.BlockSpec(memory_space=pltpu.SMEM)],
+                in_specs=[HBM, pl.BlockSpec(memory_space=pltpu.SMEM)],
                 out_specs=(VMEM,) * (2 * z_size),
                 out_shape=(pltpu.VMEM(shape, BF16),) * (2 * z_size),
                 scratch_shapes=[
@@ -210,40 +228,35 @@
                 [VMEM] * len(args),
                 [sds((n, 2, points, rows), F32)],
                 args,
-                8,
                 alias=None if first else {len(args) - 1: 0},
             )
         back = total.reshape(2 * n, n_f, own, rows).transpose(1, 0, 2, 3)
         back = lax.all_to_all(back, "freq", split_axis=0, concat_axis=0, tiled=True)
         return back.reshape(n_rows, own * rows)
 
-    def mute(back, last, add, keep):
-        outs = [sds((own * rows, samples), F32)] if last or keep else []
-        outs += [] if last else [sds((n_rows, own * rows), F32)]
-        args = (scale, limit, back, th, tl)
-        if add:
-            args = (*args, traces if last else start)
-        got = call(
-            functools.partial(mute_body, last, add, keep), [VMEM] * len(args), outs, args, 8
-        )
-        return got
+    def mute(back, last, base):
+        outs = [sds((own * rows, samples) if last else (n_rows, own * rows), F32)]
+        args = (scale, limit, back, th, tl) + (() if base is None else (base,))
+        body = functools.partial(mute_body, last, base is not None)
+        return call(body, [VMEM] * len(args), outs, args)[0]
 
     field = start
     for iteration in range(ITERS):
         final = iteration == ITERS - 1
-        got = mute(product(field, 1.0), False, False, final)
-        downgoing, field = got if final else (None, got[0])
-        got = mute(product(field, -1.0), final, True, False)
-        field = got[0]
+        back = product(field, 1.0)
+        field = mute(back, False, None)
+        if final:
+            downgoing = mute(back, True, None)
+        back = product(field, -1.0)
+        field = mute(back, final, traces if final else start)
     return field.reshape(focus_start.shape), downgoing.reshape(focus_start.shape)
 
 
 def solution(mesh):
     in_specs = (P(None, "freq", "rcv", None), P("freq", "rcv", None), P("freq", "rcv"), P())
     out_specs = (P("freq", "rcv", None), P("freq", "rcv", None))
-    z_size = mesh.shape["rcv"]
     return jax.shard_map(
-        functools.partial(body, z_size),
+        functools.partial(body, mesh.shape["rcv"]),
         mesh=mesh,
         in_specs=in_specs,
         out_specs=out_specs,

time: 200 us -> 188 us (0.940)
  starting transfers between devices: 45.6 us -> 35.8 us
  blocking collectives: 77.1 us -> 67.8 us
  waiting for transfers between devices: 23.7 us -> 30.3 us
    ppermute x20 -> x18, starting transfers between devices: 45.6 us -> 32.3 us  [shift(): return lax.ppermute(x, 'rcv', [(i, i ^ d) for i in range(z_size)])]
    all_to_all x4 -> x3, blocking collectives: 37.3 us -> 27.9 us  [product(): back = lax.all_to_all(back, 'freq', split_axis=0, concat_axis=0, tiled=True)]
    all_to_all x0 -> x1, waiting for transfers between devices: none -> 5.56 us  [product(): back = lax.all_to_all(back, 'freq', split_axis=0, concat_axis=0, tiled=True)]
    all_to_all x0 -> x1, starting transfers between devices: none -> 3.41 us  [product(): back = lax.all_to_all(back, 'freq', split_axis=0, concat_axis=0, tiled=True)]
    ppermute x20 -> x18, waiting for transfers between devices: 23.7 us -> 24.8 us  [shift(): return lax.ppermute(x, 'rcv', [(i, i ^ d) for i in range(z_size)])]
    pallas_call x21 -> x22, Pallas kernels: 30 us -> 29.7 us  [call(): pl.pallas_call(body, in_specs=ins, out_specs=tuple((VMEM for _ in outs)),...]
  transfers between devices with their start and end apart: 20 -> 19, of which waited for: 8 -> 9; matrix products, arithmetic and copies ran while one was open for 0% -> 0% of each run, Pallas kernels for 19% -> 21%
where the time goes in v3:
time: 188 us; the launch traced here: 187 us
  blocking collectives  67.8 us (36%)
  Pallas kernels  48.7 us (26%)
  starting transfers between devices  35.8 us (19%)
  waiting for transfers between devices  30.3 us (16%)
  local copies, waits for them, and re-layouts  4.15 us (2%)
    all_to_all x4, blocking collectives, product(): x = lax.all_to_all(s, 'freq', split_axis=0, concat_axis=0, tiled=True)  39.8 us
    ppermute x18, starting transfers between devices, shift(): return lax.ppermute(x, 'rcv', [(i, i ^ d) for i in range(z_size)])  32.3 us
    pallas_call x22, Pallas kernels, call(): pl.pallas_call(body, in_specs=ins, out_specs=tuple((VMEM for _ in outs)),...  29.7 us
    all_to_all x3, blocking collectives, product(): back = lax.all_to_all(back, 'freq', split_axis=0, concat_axis=0, tiled=True)  27.9 us
    ppermute x18, waiting for transfers between devices, shift(): return lax.ppermute(x, 'rcv', [(i, i ^ d) for i in range(z_size)])  24.8 us
    pallas_call x1, Pallas kernels, product(): pl.pallas_call(functools.partial(hold_body, z_size), in_specs=[HBM, pl.Bl...  19 us
    all_to_all x1, waiting for transfers between devices, product(): back = lax.all_to_all(back, 'freq', split_axis=0, concat_axis=0, tiled=True)  5.56 us
  transfers between devices with their start and end apart: 19, of which 9 were waited for; matrix products, arithmetic and copies ran while one was open for 0% of the time, Pallas kernels for 21%

profile of v3, /device:TPU:0, one launch (start us, length us, event | category | flops | bytes accessed | tf_op | source)
XLA Modules:
  0.0 187.5 jit_solution(13719753724319722877)
XLA Ops:
  4.2 11.9 %all_to_all.40 = f32[8,32,1,256]{3,1,2,0:T(8,128)S(1)} all-to-all(f32[8,32,1,256]{3,1,2,0:T(8,128)S(1)} %bitcast.93), channel_id=1, replica_groups=mesh['freq'=8,'rcv'=4] {'freq'}, dimensions={0} | all-to-all | bytes 524288 | tf_op jit(solution)/shard_map/all_to_all | solution.py:203
  16.3 1.6 collective-permute-start.2
  17.9 2.6 %collective-permute-start.1 = (f32[16,2,8,256]{3,2,1,0:T(8,128)S(1)}, f32[16,2,8,256]{3,2,1,0:T(8,128)S(1)}, u32[]{:S(2)}, u32[]{:S(2)}) collective-permute-start(f32[16,2,8,256]{3,2,1,0:T(8,128)S(1)} %bitcast.87), channel_id=1, source_target_pairs={{0,2},{1,3},{2,0},{3,1},{4,6},{5,7},{6,4},{7,5},{8,10},{9,11},{10,... | collective-permute-start | bytes 786440 | tf_op jit(solution)/shard_map/ppermute | solution.py:186
  20.7 19.0 %shard_map.60 = (bf16[2,16,256,256]{3,2,1,0:T(8,128)(2,1)S(1)}, bf16[2,16,256,256]{3,2,1,0:T(8,128)(2,1)S(1)}, bf16[2,16,256,256]{3,2,1,0:T(8,128)(2,1)S(1)}, bf...) custom-call(f32[2,16,256,1024]{3,2,1,0:T(8,128)} %kernel.1, ...), custom_call_target="tpu_custom_call" | custom-call | tf_op jit(solution)/shard_map/pallas_call | solution.py:208
  39.7 1.4 shard_map.61.rest_3_
  41.1 1.5 shard_map.62.rest_3_
  42.6 1.4 shard_map.63.rest_3_
  44.1 1.4 shard_map.64
  45.6 9.3 %all_to_all.41 = f32[8,32,1,256]{3,1,2,0:T(8,128)S(1)} all-to-all(f32[8,32,1,256]{3,1,2,0:T(8,128)S(1)} %bitcast.98), channel_id=1, replica_groups=mesh['freq'=8,'rcv'=4] {'freq'}, dimensions={0} | all-to-all | bytes 524288 | tf_op jit(solution)/shard_map/all_to_all | solution.py:234
  56.0 9.3 %all_to_all.42 = f32[8,32,1,256]{3,1,2,0:T(8,128)S(1)} all-to-all(f32[8,32,1,256]{3,1,2,0:T(8,128)S(1)} %bitcast.91), channel_id=1, replica_groups=mesh['freq'=8,'rcv'=4] {'freq'}, dimensions={0} | all-to-all | bytes 524288 | tf_op jit(solution)/shard_map/all_to_all | solution.py:203
  66.3 3.5 %collective-permute-start.3 = (f32[8,2,8,256]{3,2,1,0:T(8,128)S(1)}, f32[8,2,8,256]{3,2,1,0:T(8,128)S(1)}, u32[]{:S(2)}, u32[]{:S(2)}) collective-permute-start(f32[8,2,8,256]{3,2,1,0:T(8,128)S(1)} %get-tuple-element.33), channel_id=1, source_target_pairs={{0,2},{1,3},{2,0},{3,1},{4,6},{5,7},{6,4},{7,5},{8,10},{9,11},{10,... | collective-permute-start | bytes 393224 | tf_op jit(solution)/shard_map/ppermute | solution.py:186
  71.3 4.5 %collective-permute-done.3.rest_4_ = f32[8,2,8,256]{3,2,1,0:T(8,128)S(1)} collective-permute-done((f32[8,2,8,256]{3,2,1,0:T(8,128)S(1)}, f32[8,2,8,256]{3,2,1,0:T(8,128)S(1)}, u32[]{:S(2)}, u32[]{:S(2)}) %collective-permute-start.3) | collective-permute-done | bytes 131104 | tf_op jit(solution)/shard_map/ppermute | solution.py:186
  75.8 5.1 %collective-permute-start.4 = (f32[8,2,8,256]{3,2,1,0:T(8,128)S(1)}, f32[8,2,8,256]{3,2,1,0:T(8,128)S(1)}, u32[]{:S(2)}, u32[]{:S(2)}) collective-permute-start(f32[8,2,8,256]{3,2,1,0:T(8,128)S(1)} %collective-permute-done.3.rest_4_), channel_id=1, source_target_pairs={{0,1},{1,0},{2,3},{3,2},{4,5},{5,4},{6,7},{7,6},{8,9},{9,8},{10,11... | collective-permute-start | bytes 393224 | tf_op jit(solution)/shard_map/ppermute | solution.py:186
  83.7 2.8 %collective-permute-done.5.rest_4_ = f32[8,2,8,256]{3,2,1,0:T(8,128)S(1)} collective-permute-done((f32[8,2,8,256]{3,2,1,0:T(8,128)S(1)}, f32[8,2,8,256]{3,2,1,0:T(8,128)S(1)}, u32[]{:S(2)}, u32[]{:S(2)}) %collective-permute-start.5) | collective-permute-done | bytes 131104 | tf_op jit(solution)/shard_map/ppermute | solution.py:186
  86.5 2.2 %shard_map.68.rest_3_ = f32[16,2,8,256]{3,2,1,0:T(8,128)S(1)} custom-call(bf16[2,16,256,256]{3,2,1,0:T(8,128)(2,1)S(1)} %get-tuple-element.20.rest_0_, bf16[2,16,256,256]{3,2,1,0:T(8,128)(2,1)S(1)} %get-tuple-element.22.rest_0_.rest_1_, bf16[2,16,256,256]{3,2,1,0:T(8,128)(2,1)S(1)} %get-tuple-element.21.rest_1_.rest_2_, ...), custom_call_target="tpu_custom_call", output_to_operand_aliasing={{}: (6, {})} | custom-call | tf_op jit(solution)/shard_map/pallas_call | solution.py:19
  89.5 9.3 %all_to_all.43 = f32[8,32,1,256]{3,1,2,0:T(8,128)S(1)} all-to-all(f32[8,32,1,256]{3,1,2,0:T(8,128)S(1)} %bitcast.99), channel_id=1, replica_groups=mesh['freq'=8,'rcv'=4] {'freq'}, dimensions={0} | all-to-all | bytes 524288 | tf_op jit(solution)/shard_map/all_to_all | solution.py:234
  99.9 9.3 %all_to_all.44 = f32[8,32,1,256]{3,1,2,0:T(8,128)S(1)} all-to-all(f32[8,32,1,256]{3,1,2,0:T(8,128)S(1)} %bitcast.95), channel_id=1, replica_groups=mesh['freq'=8,'rcv'=4] {'freq'}, dimensions={0} | all-to-all | bytes 524288 | tf_op jit(solution)/shard_map/all_to_all | solution.py:203
  110.0 2.5 %collective-permute-start.8 = (f32[8,2,8,256]{3,2,1,0:T(8,128)S(1)}, f32[8,2,8,256]{3,2,1,0:T(8,128)S(1)}, u32[]{:S(2)}, u32[]{:S(2)}) collective-permute-start(f32[8,2,8,256]{3,2,1,0:T(8,128)S(1)} %get-tuple-element.31), channel_id=1, source_target_pairs={{0,2},{1,3},{2,0},{3,1},{4,6},{5,7},{6,4},{7,5},{8,10},{9,11},{10,... | collective-permute-start | bytes 393224 | tf_op jit(solution)/shard_map/ppermute | solution.py:186
  114.4 5.1 %collective-permute-done.8.rest_4_ = f32[8,2,8,256]{3,2,1,0:T(8,128)S(1)} collective-permute-done((f32[8,2,8,256]{3,2,1,0:T(8,128)S(1)}, f32[8,2,8,256]{3,2,1,0:T(8,128)S(1)}, u32[]{:S(2)}, u32[]{:S(2)}) %collective-permute-start.8) | collective-permute-done | bytes 131104 | tf_op jit(solution)/shard_map/ppermute | solution.py:186
  119.5 3.5 %collective-permute-start.9 = (f32[8,2,8,256]{3,2,1,0:T(8,128)S(1)}, f32[8,2,8,256]{3,2,1,0:T(8,128)S(1)}, u32[]{:S(2)}, u32[]{:S(2)}) collective-permute-start(f32[8,2,8,256]{3,2,1,0:T(8,128)S(1)} %collective-permute-done.8.rest_4_), channel_id=1, source_target_pairs={{0,1},{1,0},{2,3},{3,2},{4,5},{5,4},{6,7},{7,6},{8,9},{9,8},{10,11... | collective-permute-start | bytes 393224 | tf_op jit(solution)/shard_map/ppermute | solution.py:186
  123.0 1.4 shard_map.71.rest_6_
  126.5 2.8 %collective-permute-done.10.rest_4_ = f32[8,2,8,256]{3,2,1,0:T(8,128)S(1)} collective-permute-done((f32[8,2,8,256]{3,2,1,0:T(8,128)S(1)}, f32[8,2,8,256]{3,2,1,0:T(8,128)S(1)}, u32[]{:S(2)}, u32[]{:S(2)}) %collective-permute-start.10) | collective-permute-done | bytes 131104 | tf_op jit(solution)/shard_map/ppermute | solution.py:186
  129.4 2.2 %shard_map.73.rest_3_ = f32[16,2,8,256]{3,2,1,0:T(8,128)S(1)} custom-call(bf16[2,16,256,256]{3,2,1,0:T(8,128)(2,1)S(1)} %get-tuple-element.20.rest_0_, bf16[2,16,256,256]{3,2,1,0:T(8,128)(2,1)S(1)} %get-tuple-element.22.rest_0_.rest_1_, bf16[2,16,256,256]{3,2,1,0:T(8,128)(2,1)S(1)} %get-tuple-element.21.rest_1_.rest_2_, ...), custom_call_target="tpu_custom_call", output_to_operand_aliasing={{}: (6, {})} | custom-call | tf_op jit(solution)/shard_map/pallas_call | solution.py:19
  132.4 9.3 %all_to_all.45 = f32[8,32,1,256]{3,1,2,0:T(8,128)S(1)} all-to-all(f32[8,32,1,256]{3,1,2,0:T(8,128)S(1)} %bitcast.100), channel_id=1, replica_groups=mesh['freq'=8,'rcv'=4] {'freq'}, dimensions={0} | all-to-all | bytes 524288 | tf_op jit(solution)/shard_map/all_to_all | solution.py:234
  142.8 9.3 %all_to_all.46 = f32[8,32,1,256]{3,1,2,0:T(8,128)S(1)} all-to-all(f32[8,32,1,256]{3,1,2,0:T(8,128)S(1)} %bitcast.92), channel_id=1, replica_groups=mesh['freq'=8,'rcv'=4] {'freq'}, dimensions={0} | all-to-all | bytes 524288 | tf_op jit(solution)/shard_map/all_to_all | solution.py:203
  152.8 2.6 %collective-permute-start.13 = (f32[8,2,8,256]{3,2,1,0:T(8,128)S(1)}, f32[8,2,8,256]{3,2,1,0:T(8,128)S(1)}, u32[]{:S(2)}, u32[]{:S(2)}) collective-permute-start(f32[8,2,8,256]{3,2,1,0:T(8,128)S(1)} %get-tuple-element.29), channel_id=1, source_target_pairs={{0,2},{1,3},{2,0},{3,1},{4,6},{5,7},{6,4},{7,5},{8,10},{9,11},{10,... | collective-permute-start | bytes 393224 | tf_op jit(solution)/shard_map/ppermute | solution.py:186
  157.3 5.1 %collective-permute-done.13.rest_4_ = f32[8,2,8,256]{3,2,1,0:T(8,128)S(1)} collective-permute-done((f32[8,2,8,256]{3,2,1,0:T(8,128)S(1)}, f32[8,2,8,256]{3,2,1,0:T(8,128)S(1)}, u32[]{:S(2)}, u32[]{:S(2)}) %collective-permute-start.13) | collective-permute-done | bytes 131104 | tf_op jit(solution)/shard_map/ppermute | solution.py:186
  162.4 3.5 %collective-permute-start.14 = (f32[8,2,8,256]{3,2,1,0:T(8,128)S(1)}, f32[8,2,8,256]{3,2,1,0:T(8,128)S(1)}, u32[]{:S(2)}, u32[]{:S(2)}) collective-permute-start(f32[8,2,8,256]{3,2,1,0:T(8,128)S(1)} %collective-permute-done.13.rest_4_), channel_id=1, source_target_pairs={{0,1},{1,0},{2,3},{3,2},{4,5},{5,4},{6,7},{7,6},{8,9},{9,8},{10,11... | collective-permute-start | bytes 393224 | tf_op jit(solution)/shard_map/ppermute | solution.py:186
  169.4 2.8 %collective-permute-done.15.rest_4_ = f32[8,2,8,256]{3,2,1,0:T(8,128)S(1)} collective-permute-done((f32[8,2,8,256]{3,2,1,0:T(8,128)S(1)}, f32[8,2,8,256]{3,2,1,0:T(8,128)S(1)}, u32[]{:S(2)}, u32[]{:S(2)}) %collective-permute-start.15) | collective-permute-done | bytes 131104 | tf_op jit(solution)/shard_map/ppermute | solution.py:186
  172.2 2.2 %shard_map.78.rest_3_ = f32[16,2,8,256]{3,2,1,0:T(8,128)S(1)} custom-call(bf16[2,16,256,256]{3,2,1,0:T(8,128)(2,1)S(1)} %get-tuple-element.20.rest_0_, bf16[2,16,256,256]{3,2,1,0:T(8,128)(2,1)S(1)} %get-tuple-element.22.rest_0_.rest_1_, bf16[2,16,256,256]{3,2,1,0:T(8,128)(2,1)S(1)} %get-tuple-element.21.rest_1_.rest_2_, ...), custom_call_target="tpu_custom_call", output_to_operand_aliasing={{}: (6, {})} | custom-call | tf_op jit(solution)/shard_map/pallas_call | solution.py:19
  176.0 3.4 %all-to-all-start.7 = ((f32[8,32,1,256]{3,1,2,0:T(8,128)}), f32[8,32,1,256]{3,1,2,0:T(8,128)S(1)}, u32[]{:S(2)}, u32[]{:S(2)}) async-start(f32[8,32,1,256]{3,1,2,0:T(8,128)} %bitcast.65), calls=%async_computation.7 | async-start | bytes 524288 | tf_op jit(solution)/shard_map/all_to_all | solution.py:234
  180.7 5.6 %all-to-all-done.7 = f32[8,32,1,256]{3,1,2,0:T(8,128)S(1)} async-done(((f32[8,32,1,256]{3,1,2,0:T(8,128)}), f32[8,32,1,256]{3,1,2,0:T(8,128)S(1)}, u32[]{:S(2)}, u32[]{:S(2)}) %all-to-all-start.7) | async-done | bytes 262176 | tf_op jit(solution)/shard_map/all_to_all | solution.py:234
  (55 shorter events, 29.1 us)
Async XLA Ops:
  0.6 1.0 copy-start
  1.7 0.7 copy-start.2
  2.4 0.7 copy-start.3
  16.3 24.9 %collective-permute-start.2 = (f32[16,2,8,256]{3,2,1,0:T(8,128)S(1)}, f32[16,2,8,256]{3,2,1,0:T(8,128)S(1)}, u32[]{:S(2)}, u32[]{:S(2)}) collective-permute-start(f32[16,2,8,256]{3,2,1,0:T(8,128)S(1)} %bitcast.86), channel_id=1, source_target_pairs={{0,1},{1,0},{2,3},{3,2},{4,5},{5,4},{6,7},{7,6},{8,9},{9,8},{10,11... | collective-permute-start | bytes 786440 | tf_op jit(solution)/shard_map/ppermute | solution.py:186
  17.9 24.7 %collective-permute-start.1 = (f32[16,2,8,256]{3,2,1,0:T(8,128)S(1)}, f32[16,2,8,256]{3,2,1,0:T(8,128)S(1)}, u32[]{:S(2)}, u32[]{:S(2)}) collective-permute-start(f32[16,2,8,256]{3,2,1,0:T(8,128)S(1)} %bitcast.87), channel_id=1, source_target_pairs={{0,2},{1,3},{2,0},{3,1},{4,6},{5,7},{6,4},{7,5},{8,10},{9,11},{10,... | collective-permute-start | bytes 786440 | tf_op jit(solution)/shard_map/ppermute | solution.py:186
  20.5 23.6 %collective-permute-start = (f32[16,2,8,256]{3,2,1,0:T(8,128)S(1)}, f32[16,2,8,256]{3,2,1,0:T(8,128)S(1)}, u32[]{:S(2)}, u32[]{:S(2)}) collective-permute-start(f32[16,2,8,256]{3,2,1,0:T(8,128)S(1)} %bitcast.88), channel_id=1, source_target_pairs={{0,3},{1,2},{2,1},{3,0},{4,7},{5,6},{6,5},{7,4},{8,11},{9,10},{10,... | collective-permute-start | bytes 786440 | tf_op jit(solution)/shard_map/ppermute | solution.py:186
  65.5 21.0 %collective-permute-start.6 = (f32[16,2,8,256]{3,2,1,0:T(8,128)S(1)}, f32[16,2,8,256]{3,2,1,0:T(8,128)S(1)}, u32[]{:S(2)}, u32[]{:S(2)}) collective-permute-start(f32[16,2,8,256]{3,2,1,0:T(8,128)S(1)} %bitcast.77), channel_id=1, source_target_pairs={{0,1},{1,0},{2,3},{3,2},{4,5},{5,4},{6,7},{7,6},{8,9},{9,8},{10,11... | collective-permute-start | bytes 786440 | tf_op jit(solution)/shard_map/ppermute | solution.py:186
  66.3 9.5 %collective-permute-start.3 = (f32[8,2,8,256]{3,2,1,0:T(8,128)S(1)}, f32[8,2,8,256]{3,2,1,0:T(8,128)S(1)}, u32[]{:S(2)}, u32[]{:S(2)}) collective-permute-start(f32[8,2,8,256]{3,2,1,0:T(8,128)S(1)} %get-tuple-element.33), channel_id=1, source_target_pairs={{0,2},{1,3},{2,0},{3,1},{4,6},{5,7},{6,4},{7,5},{8,10},{9,11},{10,... | collective-permute-start | bytes 393224 | tf_op jit(solution)/shard_map/ppermute | solution.py:186
  69.8 12.6 %collective-permute-start.7 = (f32[8,2,8,256]{3,2,1,0:T(8,128)S(1)}, f32[8,2,8,256]{3,2,1,0:T(8,128)S(1)}, u32[]{:S(2)}, u32[]{:S(2)}) collective-permute-start(f32[8,2,8,256]{3,2,1,0:T(8,128)S(1)} %get-tuple-element.32), channel_id=1, source_target_pairs={{0,3},{1,2},{2,1},{3,0},{4,7},{5,6},{6,5},{7,4},{8,11},{9,10},{10,... | collective-permute-start | bytes 393224 | tf_op jit(solution)/shard_map/ppermute | solution.py:186
  70.0 16.5 %collective-permute-start.5 = (f32[8,2,8,256]{3,2,1,0:T(8,128)S(1)}, f32[8,2,8,256]{3,2,1,0:T(8,128)S(1)}, u32[]{:S(2)}, u32[]{:S(2)}) collective-permute-start(f32[8,2,8,256]{3,2,1,0:T(8,128)S(1)} %get-tuple-element.32), channel_id=1, source_target_pairs={{0,2},{1,3},{2,0},{3,1},{4,6},{5,7},{6,4},{7,5},{8,10},{9,11},{10,... | collective-permute-start | bytes 393224 | tf_op jit(solution)/shard_map/ppermute | solution.py:186
  75.8 12.9 %collective-permute-start.4 = (f32[8,2,8,256]{3,2,1,0:T(8,128)S(1)}, f32[8,2,8,256]{3,2,1,0:T(8,128)S(1)}, u32[]{:S(2)}, u32[]{:S(2)}) collective-permute-start(f32[8,2,8,256]{3,2,1,0:T(8,128)S(1)} %collective-permute-done.3.rest_4_), channel_id=1, source_target_pairs={{0,1},{1,0},{2,3},{3,2},{4,5},{5,4},{6,7},{7,6},{8,9},{9,8},{10,11... | collective-permute-start | bytes 393224 | tf_op jit(solution)/shard_map/ppermute | solution.py:186
  109.4 20.0 %collective-permute-start.11 = (f32[16,2,8,256]{3,2,1,0:T(8,128)S(1)}, f32[16,2,8,256]{3,2,1,0:T(8,128)S(1)}, u32[]{:S(2)}, u32[]{:S(2)}) collective-permute-start(f32[16,2,8,256]{3,2,1,0:T(8,128)S(1)} %bitcast.80), channel_id=1, source_target_pairs={{0,1},{1,0},{2,3},{3,2},{4,5},{5,4},{6,7},{7,6},{8,9},{9,8},{10,11... | collective-permute-start | bytes 786440 | tf_op jit(solution)/shard_map/ppermute | solution.py:186
  110.0 9.6 %collective-permute-start.8 = (f32[8,2,8,256]{3,2,1,0:T(8,128)S(1)}, f32[8,2,8,256]{3,2,1,0:T(8,128)S(1)}, u32[]{:S(2)}, u32[]{:S(2)}) collective-permute-start(f32[8,2,8,256]{3,2,1,0:T(8,128)S(1)} %get-tuple-element.31), channel_id=1, source_target_pairs={{0,2},{1,3},{2,0},{3,1},{4,6},{5,7},{6,4},{7,5},{8,10},{9,11},{10,... | collective-permute-start | bytes 393224 | tf_op jit(solution)/shard_map/ppermute | solution.py:186
  112.5 12.7 %collective-permute-start.12 = (f32[8,2,8,256]{3,2,1,0:T(8,128)S(1)}, f32[8,2,8,256]{3,2,1,0:T(8,128)S(1)}, u32[]{:S(2)}, u32[]{:S(2)}) collective-permute-start(f32[8,2,8,256]{3,2,1,0:T(8,128)S(1)} %get-tuple-element.30), channel_id=1, source_target_pairs={{0,3},{1,2},{2,1},{3,0},{4,7},{5,6},{6,5},{7,4},{8,11},{9,10},{10,... | collective-permute-start | bytes 393224 | tf_op jit(solution)/shard_map/ppermute | solution.py:186
  113.9 15.5 %collective-permute-start.10 = (f32[8,2,8,256]{3,2,1,0:T(8,128)S(1)}, f32[8,2,8,256]{3,2,1,0:T(8,128)S(1)}, u32[]{:S(2)}, u32[]{:S(2)}) collective-permute-start(f32[8,2,8,256]{3,2,1,0:T(8,128)S(1)} %get-tuple-element.30), channel_id=1, source_target_pairs={{0,2},{1,3},{2,0},{3,1},{4,6},{5,7},{6,4},{7,5},{8,10},{9,11},{10,... | collective-permute-start | bytes 393224 | tf_op jit(solution)/shard_map/ppermute | solution.py:186
  119.5 12.0 %collective-permute-start.9 = (f32[8,2,8,256]{3,2,1,0:T(8,128)S(1)}, f32[8,2,8,256]{3,2,1,0:T(8,128)S(1)}, u32[]{:S(2)}, u32[]{:S(2)}) collective-permute-start(f32[8,2,8,256]{3,2,1,0:T(8,128)S(1)} %collective-permute-done.8.rest_4_), channel_id=1, source_target_pairs={{0,1},{1,0},{2,3},{3,2},{4,5},{5,4},{6,7},{7,6},{8,9},{9,8},{10,11... | collective-permute-start | bytes 393224 | tf_op jit(solution)/shard_map/ppermute | solution.py:186
  152.3 19.9 %collective-permute-start.16 = (f32[16,2,8,256]{3,2,1,0:T(8,128)S(1)}, f32[16,2,8,256]{3,2,1,0:T(8,128)S(1)}, u32[]{:S(2)}, u32[]{:S(2)}) collective-permute-start(f32[16,2,8,256]{3,2,1,0:T(8,128)S(1)} %bitcast.74), channel_id=1, source_target_pairs={{0,1},{1,0},{2,3},{3,2},{4,5},{5,4},{6,7},{7,6},{8,9},{9,8},{10,11... | collective-permute-start | bytes 786440 | tf_op jit(solution)/shard_map/ppermute | solution.py:186
  152.8 9.5 %collective-permute-start.13 = (f32[8,2,8,256]{3,2,1,0:T(8,128)S(1)}, f32[8,2,8,256]{3,2,1,0:T(8,128)S(1)}, u32[]{:S(2)}, u32[]{:S(2)}) collective-permute-start(f32[8,2,8,256]{3,2,1,0:T(8,128)S(1)} %get-tuple-element.29), channel_id=1, source_target_pairs={{0,2},{1,3},{2,0},{3,1},{4,6},{5,7},{6,4},{7,5},{8,10},{9,11},{10,... | collective-permute-start | bytes 393224 | tf_op jit(solution)/shard_map/ppermute | solution.py:186
  155.5 12.6 %collective-permute-start.17 = (f32[8,2,8,256]{3,2,1,0:T(8,128)S(1)}, f32[8,2,8,256]{3,2,1,0:T(8,128)S(1)}, u32[]{:S(2)}, u32[]{:S(2)}) collective-permute-start(f32[8,2,8,256]{3,2,1,0:T(8,128)S(1)} %get-tuple-element.28), channel_id=1, source_target_pairs={{0,3},{1,2},{2,1},{3,0},{4,7},{5,6},{6,5},{7,4},{8,11},{9,10},{10,... | collective-permute-start | bytes 393224 | tf_op jit(solution)/shard_map/ppermute | solution.py:186
  156.7 15.5 %collective-permute-start.15 = (f32[8,2,8,256]{3,2,1,0:T(8,128)S(1)}, f32[8,2,8,256]{3,2,1,0:T(8,128)S(1)}, u32[]{:S(2)}, u32[]{:S(2)}) collective-permute-start(f32[8,2,8,256]{3,2,1,0:T(8,128)S(1)} %get-tuple-element.28), channel_id=1, source_target_pairs={{0,2},{1,3},{2,0},{3,1},{4,6},{5,7},{6,4},{7,5},{8,10},{9,11},{10,... | collective-permute-start | bytes 393224 | tf_op jit(solution)/shard_map/ppermute | solution.py:186
  162.4 12.0 %collective-permute-start.14 = (f32[8,2,8,256]{3,2,1,0:T(8,128)S(1)}, f32[8,2,8,256]{3,2,1,0:T(8,128)S(1)}, u32[]{:S(2)}, u32[]{:S(2)}) collective-permute-start(f32[8,2,8,256]{3,2,1,0:T(8,128)S(1)} %collective-permute-done.13.rest_4_), channel_id=1, source_target_pairs={{0,1},{1,0},{2,3},{3,2},{4,5},{5,4},{6,7},{7,6},{8,9},{9,8},{10,11... | collective-permute-start | bytes 393224 | tf_op jit(solution)/shard_map/ppermute | solution.py:186
  174.4 11.8 %copy-start.1 = (f32[1,256,512]{2,1,0:T(8,128)S(1)}, f32[1,256,512]{2,1,0:T(8,128)}, u32[]{:S(2)}) copy-start(f32[1,256,512]{2,1,0:T(8,128)} %param.5) | copy-start | bytes 1572868
  176.0 10.3 %all-to-all-start.7 = ((f32[8,32,1,256]{3,1,2,0:T(8,128)}), f32[8,32,1,256]{3,1,2,0:T(8,128)S(1)}, u32[]{:S(2)}, u32[]{:S(2)}) async-start(f32[8,32,1,256]{3,1,2,0:T(8,128)} %bitcast.65), calls=%async_computation.7 | async-start | bytes 524288 | tf_op jit(solution)/shard_map/all_to_all | solution.py:234

commit v4 on v3

--- a/solution.py
+++ b/solution.py
@@ -92,23 +92,24 @@
 
 def hold_body(blocks, kernel, place, *rest):
     *outs, buf, sem = rest
-    n = kernel.shape[1]
-    rows = kernel.shape[2]
-
-    def copy(k, slot):
+    n, rows = kernel.shape[1:3]
+    slots = buf.shape[0]
+
+    def copy(k):
+        slot = lax.rem(k, slots)
         return pltpu.make_async_copy(kernel.at[:, k], buf.at[slot], sem.at[slot])
 
-    copy(0, 0).start()
+    for k in range(min(slots - 1, n)):
+        copy(k).start()
 
     @pl.loop(0, n)
     def _(k):
-        slot = lax.rem(k, 2)
-
-        @pl.when(k + 1 < n)
+        @pl.when(k + slots - 1 < n)
         def _():
-            copy(k + 1, 1 - slot).start()
-
-        copy(k, slot).wait()
+            copy(k + slots - 1).start()
+
+        copy(k).wait()
+        slot = lax.rem(k, slots)
         for b in range(blocks):
             col = pl.multiple_of(jnp.bitwise_xor(place[0], b) * rows, rows)
             for c in range(2):
@@ -171,7 +172,10 @@
         [HBM] * 3,
         [sds((n_rows, samples), BF16)] * 2
         + [sds((n_rows, 1), F32), sds((own * rows, 1), jnp.int32), sds((n_rows, own * rows), F32)],
-        (freq_order.reshape(1, -1), onset.reshape(1, -1), traces),
+        [
+            pltpu.with_memory_space_constraint(x, pltpu.HBM)
+            for x in (freq_order.reshape(1, -1), onset.reshape(1, -1), traces)
+        ],
         scratch=[
             pltpu.VMEM((1, n_rows // 2), jnp.int32),
             pltpu.VMEM((1, own * rows), jnp.int32),
@@ -185,37 +189,43 @@
     def shift(x, d):
         return lax.ppermute(x, "rcv", [(i, i ^ d) for i in range(z_size)])
 
-    def gather(x, relay):
+    def gather(x):
         half = n // 2
-        if z_size != 4 or n % 2 or not relay:
+        if z_size != 4 or n % 2:
             return [[(0, 0, x)]] + [[(d, 0, shift(x, d))] for d in range(1, z_size)]
         low, high = x[:half], x[half:]
         b0 = shift(low, 2)
+        a = shift(x, 1)
         c1 = shift(high, 3)
         b1 = shift(high, 2)
-        a = shift(x, 1)
         c0 = shift(b0, 1)
-        return [[(0, 0, x)], [(2, 0, b0), (3, half, c1)], [(2, half, b1), (1, 0, a)], [(3, 0, c0)]]
+        groups = [[(0, 0, x)], [(2, 0, b0)], [(3, half, c1)]]
+        late = [[(1, 0, a)], [(2, half, b1)]]
+        relayed = [[(3, 0, c0)]]
+        return groups + (late + relayed if held is None else relayed + late)
+
+    def hold():
+        shape = (2, n, rows, rows)
+        return pl.pallas_call(
+            functools.partial(hold_body, z_size),
+            in_specs=[HBM, pl.BlockSpec(memory_space=pltpu.SMEM)],
+            out_specs=(VMEM,) * (2 * z_size),
+            out_shape=(pltpu.VMEM(shape, BF16),) * (2 * z_size),
+            scratch_shapes=[
+                pltpu.VMEM((4, 2, rows, receivers), F32),
+                pltpu.SemaphoreType.DMA((4,)),
+            ],
+            compiler_params=pltpu.CompilerParams(vmem_limit_bytes=12 << 20),
+        )(kernel, place)
 
     def product(spectrum, parity):
         nonlocal held
         s = spectrum.reshape(n_f, 2 * n, own, rows)
         x = lax.all_to_all(s, "freq", split_axis=0, concat_axis=0, tiled=True)
         x = x.reshape(n_f, n, 2, own, rows).transpose(1, 2, 0, 3, 4).reshape(n, 2, points, rows)
-        groups = gather(x, held is not None)
+        groups = gather(x)
         if held is None:
-            shape = (2, n, rows, rows)
-            held = pl.pallas_call(
-                functools.partial(hold_body, z_size),
-                in_specs=[HBM, pl.BlockSpec(memory_space=pltpu.SMEM)],
-                out_specs=(VMEM,) * (2 * z_size),
-                out_shape=(pltpu.VMEM(shape, BF16),) * (2 * z_size),
-                scratch_shapes=[
-                    pltpu.VMEM((2, 2, rows, receivers), F32),
-                    pltpu.SemaphoreType.DMA((2,)),
-                ],
-                compiler_params=pltpu.CompilerParams(vmem_limit_bytes=9 << 20),
-            )(kernel, place)
+            held = hold()
         total = None
         for group in groups:
             args = [held[2 * b + h] for h in (0, 1) for b, _, _ in group]

time: 188 us -> 189 us (level)
  waiting for transfers between devices: 30.3 us -> 38.3 us
  Pallas kernels: 48.7 us -> 42.1 us
  local copies, waits for them, and re-layouts: 4.15 us -> 1.81 us
    ppermute x18 -> x20, waiting for transfers between devices: 24.8 us -> 32.8 us  [shift(): return lax.ppermute(x, 'rcv', [(i, i ^ d) for i in range(z_size)])]
    pallas_call x1, Pallas kernels: 19 us -> 11.5 us  [hold(): pl.pallas_call(functools.partial(hold_body, z_size), in_specs=[HBM, pl.Bl...]
    unnamed x8 -> x2, local copies, waits for them, and re-layouts: 2.38 us -> 0.01 us
    ppermute x18 -> x20, starting transfers between devices: 32.3 us -> 34 us  [shift(): return lax.ppermute(x, 'rcv', [(i, i ^ d) for i in range(z_size)])]
    pallas_call x22 -> x30, Pallas kernels: 29.7 us -> 30.6 us  [call(): pl.pallas_call(body, in_specs=ins, out_specs=tuple((VMEM for _ in outs)),...]
  transfers between devices with their start and end apart: 19 -> 21, of which waited for: 9 -> 11; matrix products, arithmetic and copies ran while one was open for 0% -> 0% of each run, Pallas kernels for 21% -> 17%
where the time goes in v4:
time: 189 us; the launch traced here: 188 us
  blocking collectives  67.8 us (36%)
  Pallas kernels  42.1 us (22%)
  waiting for transfers between devices  38.3 us (20%)
  starting transfers between devices  37.5 us (20%)
    all_to_all x4, blocking collectives, product(): x = lax.all_to_all(s, 'freq', split_axis=0, concat_axis=0, tiled=True)  39.8 us
    ppermute x20, starting transfers between devices, shift(): return lax.ppermute(x, 'rcv', [(i, i ^ d) for i in range(z_size)])  34 us
    ppermute x20, waiting for transfers between devices, shift(): return lax.ppermute(x, 'rcv', [(i, i ^ d) for i in range(z_size)])  32.8 us
    pallas_call x30, Pallas kernels, call(): pl.pallas_call(body, in_specs=ins, out_specs=tuple((VMEM for _ in outs)),...  30.6 us
    all_to_all x3, blocking collectives, product(): back = lax.all_to_all(back, 'freq', split_axis=0, concat_axis=0, tiled=True)  27.9 us
    pallas_call x1, Pallas kernels, hold(): pl.pallas_call(functools.partial(hold_body, z_size), in_specs=[HBM, pl.Bl...  11.5 us
    all_to_all x1, waiting for transfers between devices, product(): back = lax.all_to_all(back, 'freq', split_axis=0, concat_axis=0, tiled=True)  5.56 us
  transfers between devices with their start and end apart: 21, of which 11 were waited for; matrix products, arithmetic and copies ran while one was open for 0% of the time, Pallas kernels for 17%

profile of v4, /device:TPU:0, one launch (start us, length us, event | category | flops | bytes accessed | tf_op | source)
XLA Modules:
  0.0 188.3 jit_solution(17102810172791265168)
XLA Ops:
  0.6 1.8 shard_map.59
  2.4 11.9 %all_to_all.40 = f32[8,32,1,256]{3,1,2,0:T(8,128)S(1)} all-to-all(f32[8,32,1,256]{3,1,2,0:T(8,128)S(1)} %bitcast.96), channel_id=1, replica_groups=mesh['freq'=8,'rcv'=4] {'freq'}, dimensions={0} | all-to-all | bytes 524288 | tf_op jit(solution)/shard_map/all_to_all | solution.py:224
  14.5 1.6 collective-permute-start.3
  16.1 2.7 %collective-permute-start = (f32[8,2,8,256]{3,2,1,0:T(8,128)S(1)}, f32[8,2,8,256]{3,2,1,0:T(8,128)S(1)}, u32[]{:S(2)}, u32[]{:S(2)}) collective-permute-start(f32[8,2,8,256]{3,2,1,0:T(8,128)S(1)} %get-tuple-element.35), channel_id=1, source_target_pairs={{0,2},{1,3},{2,0},{3,1},{4,6},{5,7},{6,4},{7,5},{8,10},{9,11},{10,... | collective-permute-start | bytes 393224 | tf_op jit(solution)/shard_map/ppermute | solution.py:190
  19.0 1.7 collective-permute-start.2
  20.7 5.0 %collective-permute-done.rest_2_ = f32[8,2,8,256]{3,2,1,0:T(8,128)S(1)} collective-permute-done((f32[8,2,8,256]{3,2,1,0:T(8,128)S(1)}, f32[8,2,8,256]{3,2,1,0:T(8,128)S(1)}, u32[]{:S(2)}, u32[]{:S(2)}) %collective-permute-start) | collective-permute-done | bytes 131104 | tf_op jit(solution)/shard_map/ppermute | solution.py:190
  25.7 4.2 %collective-permute-start.1 = (f32[8,2,8,256]{3,2,1,0:T(8,128)S(1)}, f32[8,2,8,256]{3,2,1,0:T(8,128)S(1)}, u32[]{:S(2)}, u32[]{:S(2)}) collective-permute-start(f32[8,2,8,256]{3,2,1,0:T(8,128)S(1)} %collective-permute-done.rest_2_), channel_id=1, source_target_pairs={{0,1},{1,0},{2,3},{3,2},{4,5},{5,4},{6,7},{7,6},{8,9},{9,8},{10,11... | collective-permute-start | bytes 393224 | tf_op jit(solution)/shard_map/ppermute | solution.py:190
  29.9 11.5 %shard_map.60 = (bf16[2,16,256,256]{3,2,1,0:T(8,128)(2,1)S(1)}, bf16[2,16,256,256]{3,2,1,0:T(8,128)(2,1)S(1)}, bf16[2,16,256,256]{3,2,1,0:T(8,128)(2,1)S(1)}, bf...) custom-call(f32[2,16,256,1024]{3,2,1,0:T(8,128)} %kernel.1, ...), custom_call_target="tpu_custom_call" | custom-call | tf_op jit(solution)/shard_map/pallas_call | solution.py:209
  47.3 9.3 %all_to_all.41 = f32[8,32,1,256]{3,1,2,0:T(8,128)S(1)} all-to-all(f32[8,32,1,256]{3,1,2,0:T(8,128)S(1)} %bitcast.100), channel_id=1, replica_groups=mesh['freq'=8,'rcv'=4] {'freq'}, dimensions={0} | all-to-all | bytes 524288 | tf_op jit(solution)/shard_map/all_to_all | solution.py:244
  57.7 9.3 %all_to_all.42 = f32[8,32,1,256]{3,1,2,0:T(8,128)S(1)} all-to-all(f32[8,32,1,256]{3,1,2,0:T(8,128)S(1)} %bitcast.94), channel_id=1, replica_groups=mesh['freq'=8,'rcv'=4] {'freq'}, dimensions={0} | all-to-all | bytes 524288 | tf_op jit(solution)/shard_map/all_to_all | solution.py:224
  67.2 3.9 %collective-permute-start.7 = (f32[8,2,8,256]{3,2,1,0:T(8,128)S(1)}, f32[8,2,8,256]{3,2,1,0:T(8,128)S(1)}, u32[]{:S(2)}, u32[]{:S(2)}) collective-permute-start(f32[8,2,8,256]{3,2,1,0:T(8,128)S(1)} %get-tuple-element.32), channel_id=1, source_target_pairs={{0,2},{1,3},{2,0},{3,1},{4,6},{5,7},{6,4},{7,5},{8,10},{9,11},{10,... | collective-permute-start | bytes 393224 | tf_op jit(solution)/shard_map/ppermute | solution.py:190
  71.1 1.5 collective-permute-start.9
  72.7 3.8 %collective-permute-done.7.rest_2_ = f32[8,2,8,256]{3,2,1,0:T(8,128)S(1)} collective-permute-done((f32[8,2,8,256]{3,2,1,0:T(8,128)S(1)}, f32[8,2,8,256]{3,2,1,0:T(8,128)S(1)}, u32[]{:S(2)}, u32[]{:S(2)}) %collective-permute-start.7) | collective-permute-done | bytes 131104 | tf_op jit(solution)/shard_map/ppermute | solution.py:190
  77.6 3.4 %collective-permute-start.5 = (f32[8,2,8,256]{3,2,1,0:T(8,128)S(1)}, f32[8,2,8,256]{3,2,1,0:T(8,128)S(1)}, u32[]{:S(2)}, u32[]{:S(2)}) collective-permute-start(f32[8,2,8,256]{3,2,1,0:T(8,128)S(1)} %get-tuple-element.33), channel_id=1, source_target_pairs={{0,2},{1,3},{2,0},{3,1},{4,6},{5,7},{6,4},{7,5},{8,10},{9,11},{10,... | collective-permute-start | bytes 393224 | tf_op jit(solution)/shard_map/ppermute | solution.py:190
  84.2 5.3 %collective-permute-done.8.rest_2_ = f32[8,2,8,256]{3,2,1,0:T(8,128)S(1)} collective-permute-done((f32[8,2,8,256]{3,2,1,0:T(8,128)S(1)}, f32[8,2,8,256]{3,2,1,0:T(8,128)S(1)}, u32[]{:S(2)}, u32[]{:S(2)}) %collective-permute-start.8) | collective-permute-done | bytes 131104 | tf_op jit(solution)/shard_map/ppermute | solution.py:190
  92.5 9.3 %all_to_all.43 = f32[8,32,1,256]{3,1,2,0:T(8,128)S(1)} all-to-all(f32[8,32,1,256]{3,1,2,0:T(8,128)S(1)} %bitcast.101), channel_id=1, replica_groups=mesh['freq'=8,'rcv'=4] {'freq'}, dimensions={0} | all-to-all | bytes 524288 | tf_op jit(solution)/shard_map/all_to_all | solution.py:244
  102.9 9.3 %all_to_all.44 = f32[8,32,1,256]{3,1,2,0:T(8,128)S(1)} all-to-all(f32[8,32,1,256]{3,1,2,0:T(8,128)S(1)} %bitcast.98), channel_id=1, replica_groups=mesh['freq'=8,'rcv'=4] {'freq'}, dimensions={0} | all-to-all | bytes 524288 | tf_op jit(solution)/shard_map/all_to_all | solution.py:224
  113.2 3.6 %collective-permute-start.14 = (f32[8,2,8,256]{3,2,1,0:T(8,128)S(1)}, f32[8,2,8,256]{3,2,1,0:T(8,128)S(1)}, u32[]{:S(2)}, u32[]{:S(2)}) collective-permute-start(f32[8,2,8,256]{3,2,1,0:T(8,128)S(1)} %get-tuple-element.31), channel_id=1, source_target_pairs={{0,3},{1,2},{2,1},{3,0},{4,7},{5,6},{6,5},{7,4},{8,11},{9,10},{10,... | collective-permute-start | bytes 393224 | tf_op jit(solution)/shard_map/ppermute | solution.py:190
  116.8 3.5 %collective-permute-done.12.rest_2_ = f32[8,2,8,256]{3,2,1,0:T(8,128)S(1)} collective-permute-done((f32[8,2,8,256]{3,2,1,0:T(8,128)S(1)}, f32[8,2,8,256]{3,2,1,0:T(8,128)S(1)}, u32[]{:S(2)}, u32[]{:S(2)}) %collective-permute-start.12) | collective-permute-done | bytes 131104 | tf_op jit(solution)/shard_map/ppermute | solution.py:190
  120.4 2.3 %collective-permute-start.10 = (f32[8,2,8,256]{3,2,1,0:T(8,128)S(1)}, f32[8,2,8,256]{3,2,1,0:T(8,128)S(1)}, u32[]{:S(2)}, u32[]{:S(2)}) collective-permute-start(f32[8,2,8,256]{3,2,1,0:T(8,128)S(1)} %get-tuple-element.31), channel_id=1, source_target_pairs={{0,2},{1,3},{2,0},{3,1},{4,6},{5,7},{6,4},{7,5},{8,10},{9,11},{10,... | collective-permute-start | bytes 393224 | tf_op jit(solution)/shard_map/ppermute | solution.py:190
  124.8 2.0 %collective-permute-done.14.rest_2_ = f32[8,2,8,256]{3,2,1,0:T(8,128)S(1)} collective-permute-done((f32[8,2,8,256]{3,2,1,0:T(8,128)S(1)}, f32[8,2,8,256]{3,2,1,0:T(8,128)S(1)}, u32[]{:S(2)}, u32[]{:S(2)}) %collective-permute-start.14) | collective-permute-done | bytes 131104 | tf_op jit(solution)/shard_map/ppermute | solution.py:190
  127.5 3.7 %collective-permute-done.13.rest_2_ = f32[8,2,8,256]{3,2,1,0:T(8,128)S(1)} collective-permute-done((f32[8,2,8,256]{3,2,1,0:T(8,128)S(1)}, f32[8,2,8,256]{3,2,1,0:T(8,128)S(1)}, u32[]{:S(2)}, u32[]{:S(2)}) %collective-permute-start.13) | collective-permute-done | bytes 131104 | tf_op jit(solution)/shard_map/ppermute | solution.py:190
  134.3 9.3 %all_to_all.45 = f32[8,32,1,256]{3,1,2,0:T(8,128)S(1)} all-to-all(f32[8,32,1,256]{3,1,2,0:T(8,128)S(1)} %bitcast.102), channel_id=1, replica_groups=mesh['freq'=8,'rcv'=4] {'freq'}, dimensions={0} | all-to-all | bytes 524288 | tf_op jit(solution)/shard_map/all_to_all | solution.py:244
  144.7 9.3 %all_to_all.46 = f32[8,32,1,256]{3,1,2,0:T(8,128)S(1)} all-to-all(f32[8,32,1,256]{3,1,2,0:T(8,128)S(1)} %bitcast.95), channel_id=1, replica_groups=mesh['freq'=8,'rcv'=4] {'freq'}, dimensions={0} | all-to-all | bytes 524288 | tf_op jit(solution)/shard_map/all_to_all | solution.py:224
  154.2 1.7 collective-permute-start.16
  156.0 2.6 %collective-permute-start.19 = (f32[8,2,8,256]{3,2,1,0:T(8,128)S(1)}, f32[8,2,8,256]{3,2,1,0:T(8,128)S(1)}, u32[]{:S(2)}, u32[]{:S(2)}) collective-permute-start(f32[8,2,8,256]{3,2,1,0:T(8,128)S(1)} %get-tuple-element.29), channel_id=1, source_target_pairs={{0,3},{1,2},{2,1},{3,0},{4,7},{5,6},{6,5},{7,4},{8,11},{9,10},{10,... | collective-permute-start | bytes 393224 | tf_op jit(solution)/shard_map/ppermute | solution.py:190
  158.6 3.5 %collective-permute-done.17.rest_2_ = f32[8,2,8,256]{3,2,1,0:T(8,128)S(1)} collective-permute-done((f32[8,2,8,256]{3,2,1,0:T(8,128)S(1)}, f32[8,2,8,256]{3,2,1,0:T(8,128)S(1)}, u32[]{:S(2)}, u32[]{:S(2)}) %collective-permute-start.17) | collective-permute-done | bytes 131104 | tf_op jit(solution)/shard_map/ppermute | solution.py:190
  162.1 2.4 %collective-permute-start.15 = (f32[8,2,8,256]{3,2,1,0:T(8,128)S(1)}, f32[8,2,8,256]{3,2,1,0:T(8,128)S(1)}, u32[]{:S(2)}, u32[]{:S(2)}) collective-permute-start(f32[8,2,8,256]{3,2,1,0:T(8,128)S(1)} %get-tuple-element.29), channel_id=1, source_target_pairs={{0,2},{1,3},{2,0},{3,1},{4,6},{5,7},{6,4},{7,5},{8,10},{9,11},{10,... | collective-permute-start | bytes 393224 | tf_op jit(solution)/shard_map/ppermute | solution.py:190
  166.7 1.9 collective-permute-done.19.rest_2_
  169.3 3.7 %collective-permute-done.18.rest_2_ = f32[8,2,8,256]{3,2,1,0:T(8,128)S(1)} collective-permute-done((f32[8,2,8,256]{3,2,1,0:T(8,128)S(1)}, f32[8,2,8,256]{3,2,1,0:T(8,128)S(1)}, u32[]{:S(2)}, u32[]{:S(2)}) %collective-permute-start.18) | collective-permute-done | bytes 131104 | tf_op jit(solution)/shard_map/ppermute | solution.py:190
  176.7 3.4 %all-to-all-start.7 = ((f32[8,32,1,256]{3,1,2,0:T(8,128)}), f32[8,32,1,256]{3,1,2,0:T(8,128)S(1)}, u32[]{:S(2)}, u32[]{:S(2)}) async-start(f32[8,32,1,256]{3,1,2,0:T(8,128)} %bitcast.69), calls=%async_computation.7 | async-start | bytes 524288 | tf_op jit(solution)/shard_map/all_to_all | solution.py:244
  181.4 5.6 %all-to-all-done.7 = f32[8,32,1,256]{3,1,2,0:T(8,128)S(1)} async-done(((f32[8,32,1,256]{3,1,2,0:T(8,128)}), f32[8,32,1,256]{3,1,2,0:T(8,128)S(1)}, u32[]{:S(2)}, u32[]{:S(2)}) %all-to-all-start.7) | async-done | bytes 262176 | tf_op jit(solution)/shard_map/all_to_all | solution.py:244
  (62 shorter events, 33.2 us)
Async XLA Ops:
  14.5 29.8 %collective-permute-start.3 = (f32[16,2,8,256]{3,2,1,0:T(8,128)S(1)}, f32[16,2,8,256]{3,2,1,0:T(8,128)S(1)}, u32[]{:S(2)}, u32[]{:S(2)}) collective-permute-start(f32[16,2,8,256]{3,2,1,0:T(8,128)S(1)} %bitcast.77), channel_id=1, source_target_pairs={{0,1},{1,0},{2,3},{3,2},{4,5},{5,4},{6,7},{7,6},{8,9},{9,8},{10,11... | collective-permute-start | bytes 786440 | tf_op jit(solution)/shard_map/ppermute | solution.py:190
  16.1 9.5 %collective-permute-start = (f32[8,2,8,256]{3,2,1,0:T(8,128)S(1)}, f32[8,2,8,256]{3,2,1,0:T(8,128)S(1)}, u32[]{:S(2)}, u32[]{:S(2)}) collective-permute-start(f32[8,2,8,256]{3,2,1,0:T(8,128)S(1)} %get-tuple-element.35), channel_id=1, source_target_pairs={{0,2},{1,3},{2,0},{3,1},{4,6},{5,7},{6,4},{7,5},{8,10},{9,11},{10,... | collective-permute-start | bytes 393224 | tf_op jit(solution)/shard_map/ppermute | solution.py:190
  18.8 24.7 %collective-permute-start.4 = (f32[8,2,8,256]{3,2,1,0:T(8,128)S(1)}, f32[8,2,8,256]{3,2,1,0:T(8,128)S(1)}, u32[]{:S(2)}, u32[]{:S(2)}) collective-permute-start(f32[8,2,8,256]{3,2,1,0:T(8,128)S(1)} %get-tuple-element.34), channel_id=1, source_target_pairs={{0,3},{1,2},{2,1},{3,0},{4,7},{5,6},{6,5},{7,4},{8,11},{9,10},{10,... | collective-permute-start | bytes 393224 | tf_op jit(solution)/shard_map/ppermute | solution.py:190
  19.0 26.7 %collective-permute-start.2 = (f32[8,2,8,256]{3,2,1,0:T(8,128)S(1)}, f32[8,2,8,256]{3,2,1,0:T(8,128)S(1)}, u32[]{:S(2)}, u32[]{:S(2)}) collective-permute-start(f32[8,2,8,256]{3,2,1,0:T(8,128)S(1)} %get-tuple-element.34), channel_id=1, source_target_pairs={{0,2},{1,3},{2,0},{3,1},{4,6},{5,7},{6,4},{7,5},{8,10},{9,11},{10,... | collective-permute-start | bytes 393224 | tf_op jit(solution)/shard_map/ppermute | solution.py:190
  25.7 20.8 %collective-permute-start.1 = (f32[8,2,8,256]{3,2,1,0:T(8,128)S(1)}, f32[8,2,8,256]{3,2,1,0:T(8,128)S(1)}, u32[]{:S(2)}, u32[]{:S(2)}) collective-permute-start(f32[8,2,8,256]{3,2,1,0:T(8,128)S(1)} %collective-permute-done.rest_2_), channel_id=1, source_target_pairs={{0,1},{1,0},{2,3},{3,2},{4,5},{5,4},{6,7},{7,6},{8,9},{9,8},{10,11... | collective-permute-start | bytes 393224 | tf_op jit(solution)/shard_map/ppermute | solution.py:190
  67.2 9.3 %collective-permute-start.7 = (f32[8,2,8,256]{3,2,1,0:T(8,128)S(1)}, f32[8,2,8,256]{3,2,1,0:T(8,128)S(1)}, u32[]{:S(2)}, u32[]{:S(2)}) collective-permute-start(f32[8,2,8,256]{3,2,1,0:T(8,128)S(1)} %get-tuple-element.32), channel_id=1, source_target_pairs={{0,2},{1,3},{2,0},{3,1},{4,6},{5,7},{6,4},{7,5},{8,10},{9,11},{10,... | collective-permute-start | bytes 393224 | tf_op jit(solution)/shard_map/ppermute | solution.py:190
  71.1 19.0 %collective-permute-start.6 = (f32[16,2,8,256]{3,2,1,0:T(8,128)S(1)}, f32[16,2,8,256]{3,2,1,0:T(8,128)S(1)}, u32[]{:S(2)}, u32[]{:S(2)}) collective-permute-start(f32[16,2,8,256]{3,2,1,0:T(8,128)S(1)} %bitcast.84), channel_id=1, source_target_pairs={{0,1},{1,0},{2,3},{3,2},{4,5},{5,4},{6,7},{7,6},{8,9},{9,8},{10,11... | collective-permute-start | bytes 786440 | tf_op jit(solution)/shard_map/ppermute | solution.py:190
  71.1 12.3 %collective-permute-start.9 = (f32[8,2,8,256]{3,2,1,0:T(8,128)S(1)}, f32[8,2,8,256]{3,2,1,0:T(8,128)S(1)}, u32[]{:S(2)}, u32[]{:S(2)}) collective-permute-start(f32[8,2,8,256]{3,2,1,0:T(8,128)S(1)} %get-tuple-element.33), channel_id=1, source_target_pairs={{0,3},{1,2},{2,1},{3,0},{4,7},{5,6},{6,5},{7,4},{8,11},{9,10},{10,... | collective-permute-start | bytes 393224 | tf_op jit(solution)/shard_map/ppermute | solution.py:190
  76.4 13.0 %collective-permute-start.8 = (f32[8,2,8,256]{3,2,1,0:T(8,128)S(1)}, f32[8,2,8,256]{3,2,1,0:T(8,128)S(1)}, u32[]{:S(2)}, u32[]{:S(2)}) collective-permute-start(f32[8,2,8,256]{3,2,1,0:T(8,128)S(1)} %collective-permute-done.7.rest_2_), channel_id=1, source_target_pairs={{0,1},{1,0},{2,3},{3,2},{4,5},{5,4},{6,7},{7,6},{8,9},{9,8},{10,11... | collective-permute-start | bytes 393224 | tf_op jit(solution)/shard_map/ppermute | solution.py:190
  77.6 14.0 %collective-permute-start.5 = (f32[8,2,8,256]{3,2,1,0:T(8,128)S(1)}, f32[8,2,8,256]{3,2,1,0:T(8,128)S(1)}, u32[]{:S(2)}, u32[]{:S(2)}) collective-permute-start(f32[8,2,8,256]{3,2,1,0:T(8,128)S(1)} %get-tuple-element.33), channel_id=1, source_target_pairs={{0,2},{1,3},{2,0},{3,1},{4,6},{5,7},{6,4},{7,5},{8,10},{9,11},{10,... | collective-permute-start | bytes 393224 | tf_op jit(solution)/shard_map/ppermute | solution.py:190
  112.4 8.0 %collective-permute-start.12 = (f32[8,2,8,256]{3,2,1,0:T(8,128)S(1)}, f32[8,2,8,256]{3,2,1,0:T(8,128)S(1)}, u32[]{:S(2)}, u32[]{:S(2)}) collective-permute-start(f32[8,2,8,256]{3,2,1,0:T(8,128)S(1)} %get-tuple-element.30), channel_id=1, source_target_pairs={{0,2},{1,3},{2,0},{3,1},{4,6},{5,7},{6,4},{7,5},{8,10},{9,11},{10,... | collective-permute-start | bytes 393224 | tf_op jit(solution)/shard_map/ppermute | solution.py:190
  112.5 19.5 %collective-permute-start.11 = (f32[16,2,8,256]{3,2,1,0:T(8,128)S(1)}, f32[16,2,8,256]{3,2,1,0:T(8,128)S(1)}, u32[]{:S(2)}, u32[]{:S(2)}) collective-permute-start(f32[16,2,8,256]{3,2,1,0:T(8,128)S(1)} %bitcast.87), channel_id=1, source_target_pairs={{0,1},{1,0},{2,3},{3,2},{4,5},{5,4},{6,7},{7,6},{8,9},{9,8},{10,11... | collective-permute-start | bytes 786440 | tf_op jit(solution)/shard_map/ppermute | solution.py:190
  113.2 13.6 %collective-permute-start.14 = (f32[8,2,8,256]{3,2,1,0:T(8,128)S(1)}, f32[8,2,8,256]{3,2,1,0:T(8,128)S(1)}, u32[]{:S(2)}, u32[]{:S(2)}) collective-permute-start(f32[8,2,8,256]{3,2,1,0:T(8,128)S(1)} %get-tuple-element.31), channel_id=1, source_target_pairs={{0,3},{1,2},{2,1},{3,0},{4,7},{5,6},{6,5},{7,4},{8,11},{9,10},{10,... | collective-permute-start | bytes 393224 | tf_op jit(solution)/shard_map/ppermute | solution.py:190
  120.4 10.9 %collective-permute-start.13 = (f32[8,2,8,256]{3,2,1,0:T(8,128)S(1)}, f32[8,2,8,256]{3,2,1,0:T(8,128)S(1)}, u32[]{:S(2)}, u32[]{:S(2)}) collective-permute-start(f32[8,2,8,256]{3,2,1,0:T(8,128)S(1)} %collective-permute-done.12.rest_2_), channel_id=1, source_target_pairs={{0,1},{1,0},{2,3},{3,2},{4,5},{5,4},{6,7},{7,6},{8,9},{9,8},{10,11... | collective-permute-start | bytes 393224 | tf_op jit(solution)/shard_map/ppermute | solution.py:190
  120.4 13.1 %collective-permute-start.10 = (f32[8,2,8,256]{3,2,1,0:T(8,128)S(1)}, f32[8,2,8,256]{3,2,1,0:T(8,128)S(1)}, u32[]{:S(2)}, u32[]{:S(2)}) collective-permute-start(f32[8,2,8,256]{3,2,1,0:T(8,128)S(1)} %get-tuple-element.31), channel_id=1, source_target_pairs={{0,2},{1,3},{2,0},{3,1},{4,6},{5,7},{6,4},{7,5},{8,10},{9,11},{10,... | collective-permute-start | bytes 393224 | tf_op jit(solution)/shard_map/ppermute | solution.py:190
  154.2 8.0 %collective-permute-start.17 = (f32[8,2,8,256]{3,2,1,0:T(8,128)S(1)}, f32[8,2,8,256]{3,2,1,0:T(8,128)S(1)}, u32[]{:S(2)}, u32[]{:S(2)}) collective-permute-start(f32[8,2,8,256]{3,2,1,0:T(8,128)S(1)} %get-tuple-element.28), channel_id=1, source_target_pairs={{0,2},{1,3},{2,0},{3,1},{4,6},{5,7},{6,4},{7,5},{8,10},{9,11},{10,... | collective-permute-start | bytes 393224 | tf_op jit(solution)/shard_map/ppermute | solution.py:190
  154.2 19.5 %collective-permute-start.16 = (f32[16,2,8,256]{3,2,1,0:T(8,128)S(1)}, f32[16,2,8,256]{3,2,1,0:T(8,128)S(1)}, u32[]{:S(2)}, u32[]{:S(2)}) collective-permute-start(f32[16,2,8,256]{3,2,1,0:T(8,128)S(1)} %bitcast.81), channel_id=1, source_target_pairs={{0,1},{1,0},{2,3},{3,2},{4,5},{5,4},{6,7},{7,6},{8,9},{9,8},{10,11... | collective-permute-start | bytes 786440 | tf_op jit(solution)/shard_map/ppermute | solution.py:190
  156.0 12.6 %collective-permute-start.19 = (f32[8,2,8,256]{3,2,1,0:T(8,128)S(1)}, f32[8,2,8,256]{3,2,1,0:T(8,128)S(1)}, u32[]{:S(2)}, u32[]{:S(2)}) collective-permute-start(f32[8,2,8,256]{3,2,1,0:T(8,128)S(1)} %get-tuple-element.29), channel_id=1, source_target_pairs={{0,3},{1,2},{2,1},{3,0},{4,7},{5,6},{6,5},{7,4},{8,11},{9,10},{10,... | collective-permute-start | bytes 393224 | tf_op jit(solution)/shard_map/ppermute | solution.py:190
  162.1 10.9 %collective-permute-start.18 = (f32[8,2,8,256]{3,2,1,0:T(8,128)S(1)}, f32[8,2,8,256]{3,2,1,0:T(8,128)S(1)}, u32[]{:S(2)}, u32[]{:S(2)}) collective-permute-start(f32[8,2,8,256]{3,2,1,0:T(8,128)S(1)} %collective-permute-done.17.rest_2_), channel_id=1, source_target_pairs={{0,1},{1,0},{2,3},{3,2},{4,5},{5,4},{6,7},{7,6},{8,9},{9,8},{10,11... | collective-permute-start | bytes 393224 | tf_op jit(solution)/shard_map/ppermute | solution.py:190
  162.1 13.1 %collective-permute-start.15 = (f32[8,2,8,256]{3,2,1,0:T(8,128)S(1)}, f32[8,2,8,256]{3,2,1,0:T(8,128)S(1)}, u32[]{:S(2)}, u32[]{:S(2)}) collective-permute-start(f32[8,2,8,256]{3,2,1,0:T(8,128)S(1)} %get-tuple-element.29), channel_id=1, source_target_pairs={{0,2},{1,3},{2,0},{3,1},{4,6},{5,7},{6,4},{7,5},{8,10},{9,11},{10,... | collective-permute-start | bytes 393224 | tf_op jit(solution)/shard_map/ppermute | solution.py:190
  175.2 11.8 %copy-start = (f32[1,256,512]{2,1,0:T(8,128)S(1)}, f32[1,256,512]{2,1,0:T(8,128)}, u32[]{:S(2)}) copy-start(f32[1,256,512]{2,1,0:T(8,128)} %param.5) | copy-start | bytes 1572868
  176.7 10.3 %all-to-all-start.7 = ((f32[8,32,1,256]{3,1,2,0:T(8,128)}), f32[8,32,1,256]{3,1,2,0:T(8,128)S(1)}, u32[]{:S(2)}, u32[]{:S(2)}) async-start(f32[8,32,1,256]{3,1,2,0:T(8,128)} %bitcast.69), calls=%async_computation.7 | async-start | bytes 524288 | tf_op jit(solution)/shard_map/all_to_all | solution.py:244
